TPU v7x, 32 devices: a whole 2x2x4 slice. The times are simulated.
32 devices in a mesh: ctx: 8 (over y, x, core), exp: 4 (over z).
Axes of the slice: x: 2, y: 2, z: 4, core: 2. Of those that a mesh axis runs over, the one named last changes fastest.
Arguments:
- queries: bfloat16 [512, 64, 512], P('ctx', 'exp'), may hold values from -17 to 17
- latent: bfloat16 [512, 512], P('ctx'), may hold values from -2 to 2
- grad_out: bfloat16 [512, 64, 512], P('ctx', 'exp'), may hold values from -6 to 6
- doc_ids: int32 [512], P('ctx'), may hold values from 0 to 5, as said below
- tokens: bfloat16 [4096, 7168], P(('ctx', 'exp')), may hold values from -6 to 6
- token_grads: bfloat16 [4096, 7168], P(('ctx', 'exp')), may hold values from -1.5 to 1.5
- gate_values: float32 [4096, 8], P(('ctx', 'exp')), may hold values from 0.3 to 3
- expert_ids: int32 [4096, 8], P(('ctx', 'exp')), may hold values from 0 to 255, as said below
- gate_order: int32 [32, 128], P(('ctx', 'exp')), may hold values from 0 to 127, each once within a row
- w_gate: bfloat16 [4, 7168, 2048], P('exp', None, 'ctx'), may hold values from -0.0625 to 0.0625
- w_up: bfloat16 [4, 7168, 2048], P('exp', None, 'ctx'), may hold values from -0.0625 to 0.0625
- w_down: bfloat16 [4, 2048, 7168], P('exp', 'ctx'), may hold values from -0.125 to 0.125
Outputs:
- d_queries: bfloat16 [512, 64, 512], P('ctx', 'exp')
- d_latent: bfloat16 [512, 512], P('ctx')
- d_tokens: bfloat16 [4096, 7168], P(('ctx', 'exp'))
- d_gates: bfloat16 [4096, 8], P(('ctx', 'exp'))
Inputs may be any that keep to these rules, and one draw needn't show every extreme that they name: `doc_ids`: never falling along the sequence; every number below 6 occurs. `expert_ids`: each row names 8 different experts. For every index of ctx some expert below 4 is named by 2 or more rows of every device at that index. `gate_order`: each row holds every number below 128 once.
All inputs are finite; a program needn't handle non-finite values.
Results may differ from a plain program's by a relative error of at most 0.02.
Values may be sent and summed in bfloat16 or wider, within the bound.
No kernel may reach another device: no remote copies, remote signals or barrier semaphores. Data moves between devices by JAX's collectives and lax.ppermute only.
A program may use at most 128 MiB of HBM per device.

v0:
```python
import functools

import jax
import jax.numpy as jnp
from jax import lax
from jax.experimental import pallas as pl
from jax.experimental.pallas import tpu as pltpu
from jax.sharding import PartitionSpec as P


SCALE_DIM = 192
CAP = 2
LANES = 128
MIB = 1 << 20
F32 = jnp.float32
BF16 = jnp.bfloat16


def exchange(array, axis, mask):
    count = lax.axis_size(axis)
    return lax.ppermute(array, axis, [(i, i ^ mask) for i in range(count)])


def turned(place):
    return (place & ~3) | ((place & 1) << 1) | ((place & 2) >> 1)


def chip_exchange(array, place):
    count = lax.axis_size("ctx")
    pairs = [(i, i ^ (2 * (turned(place) if i & 1 else place))) for i in range(count)]
    return lax.ppermute(array, "ctx", pairs)


def core_exchange(array):
    return exchange(array, "ctx", 1)


def vmem_spec():
    return pl.BlockSpec(memory_space=pltpu.VMEM)


def hbm_spec():
    return pl.BlockSpec(memory_space=pltpu.HBM)


def nbytes(shape, dtype):
    total = jnp.dtype(dtype).itemsize
    for size in shape:
        total *= size
    return total


def call(body, outs, args, in_specs, scratch, limit, flops=0, out_specs=None):
    moved = sum(nbytes(a.shape, a.dtype) for a in args)
    moved += sum(nbytes(o.shape, o.dtype) for o in outs)
    args = [
        pltpu.with_memory_space_constraint(a, pltpu.HBM) if s.memory_space == pltpu.HBM else a
        for a, s in zip(args, in_specs)
    ]
    return pl.pallas_call(
        body,
        out_shape=outs,
        in_specs=in_specs,
        out_specs=out_specs or [vmem_spec() for _ in outs],
        scratch_shapes=scratch,
        compiler_params=pltpu.CompilerParams(vmem_limit_bytes=limit),
        cost_estimate=pl.CostEstimate(flops=flops, bytes_accessed=moved, transcendentals=0),
    )(*args)


def slot_experts(shape):
    slot = lax.broadcasted_iota(jnp.int32, shape, 0)
    return (slot >> (CAP.bit_length() - 1)) ^ lax.axis_index("exp")


def route_body(n_exp, ids_hbm, order_hbm, gates_hbm, tok_hbm, grad_hbm, *rest):
    msgs = rest[:n_exp]
    weight_ref, chosen_ref, ids_ref, order_ref, gates_ref, held, sems = rest[n_exp:]
    pieces = 2
    width = held.shape[2]
    piece = width // pieces
    small = [
        pltpu.make_async_copy(src, dst, sems.at[i])
        for i, (src, dst) in enumerate(
            ((ids_hbm, ids_ref), (order_hbm, order_ref), (gates_hbm, gates_ref))
        )
    ]
    large = [
        pltpu.make_async_copy(
            src.at[:, pl.ds(c * piece, piece)],
            held.at[i, :, pl.ds(c * piece, piece)],
            sems.at[3 + i * pieces + c],
        )
        for c in range(pieces)
        for i, src in enumerate((tok_hbm, grad_hbm))
    ]
    for copy in small + large:
        copy.start()
    for copy in small:
        copy.wait()
    top, rows = ids_ref.shape
    shape = (n_exp * CAP, rows)
    expert = slot_experts(shape)
    ids = ids_ref[...]
    gates = gates_ref[...]
    hits = jnp.zeros(shape, F32)
    mass = jnp.zeros(shape, F32)
    for j in range(top):
        match = ids[j : j + 1] == expert
        hits = hits + jnp.where(match, 1.0, 0.0)
        mass = mass + jnp.where(match, gates[j : j + 1], 0.0)
    order = jnp.broadcast_to(order_ref[...].astype(F32), (rows, rows))
    earlier = jnp.where(order.T < order, 1.0, 0.0).astype(BF16)
    ranks = jnp.dot(hits.astype(BF16), earlier, preferred_element_type=F32)
    slot = (lax.broadcasted_iota(jnp.int32, shape, 0) & (CAP - 1)).astype(F32)
    chosen = jnp.where((hits == 1.0) & (ranks == slot), 1.0, 0.0)
    weight_ref[...] = chosen * mass
    chosen_ref[...] = chosen
    pick = chosen.astype(BF16)
    for c in range(pieces):
        large[2 * c].wait()
        large[2 * c + 1].wait()
        cols = pl.ds(c * piece, piece)
        tok = jnp.dot(pick, held[0, :, cols], preferred_element_type=F32)
        grad = jnp.dot(pick, held[1, :, cols], preferred_element_type=F32)
        for k in range(n_exp):
            span = slice(k * CAP, (k + 1) * CAP)
            msgs[k][:, cols] = jnp.concatenate([tok[span], grad[span]], axis=0).astype(BF16)


def route(expert_ids, gate_order, gate_values, tokens, token_grads, n_exp):
    rows, width = tokens.shape
    top = expert_ids.shape[1]
    outs = [jax.ShapeDtypeStruct((2 * CAP, width), BF16) for _ in range(n_exp)]
    outs += [jax.ShapeDtypeStruct((n_exp * CAP, rows), F32)] * 2
    res = call(
        functools.partial(route_body, n_exp),
        outs,
        (expert_ids.T, gate_order, gate_values.T, tokens, token_grads),
        [hbm_spec()] * 5,
        [
            pltpu.VMEM((top, rows), jnp.int32),
            pltpu.VMEM((1, rows), jnp.int32),
            pltpu.VMEM((top, rows), F32),
            pltpu.VMEM((2, rows, width), BF16),
            pltpu.SemaphoreType.DMA((7,)),
        ],
        12 * MIB,
        flops=4 * n_exp * CAP * rows * width,
    )
    return res[:n_exp], res[n_exp], res[n_exp + 1]


def attention_body(n_ctx, heads, row_block, *refs):
    q_ref, go_ref = refs[:2]
    blocks = refs[2 : 2 + n_ctx]
    w_hbm = refs[2 + n_ctx : 5 + n_ctx]
    dq_hbm, even_ref, odd_ref = refs[5 + n_ctx : 8 + n_ctx]
    w_vmem = refs[8 + n_ctx : 11 + n_ctx]
    lat, dq, dq_sems, w_sems = refs[11 + n_ctx :]
    fetches = [
        pltpu.make_async_copy(src.at[0], dst, w_sems.at[i])
        for i, (src, dst) in enumerate(zip(w_hbm, w_vmem))
    ]
    for fetch in fetches:
        fetch.start()
    per = blocks[0].shape[0]
    rows, width = q_ref.shape
    scale = SCALE_DIM ** (-0.5)
    keydoc = []
    for i, block in enumerate(blocks):
        lat[i * per : (i + 1) * per, :] = block[:, :width]
        keydoc.append(block[:, width:].astype(F32))
    keydoc = jnp.concatenate(keydoc, axis=0)
    reps = row_block // LANES
    if reps > 1:
        keydoc = jnp.concatenate([keydoc] * reps, axis=1)
    keys = lat[...]
    nt = (((1,), (1,)), ((), ()))
    tn = (((0,), (0,)), ((), ()))
    owner = lax.broadcasted_iota(jnp.int32, (per, row_block), 0)
    col = lax.broadcasted_iota(jnp.int32, (per, row_block), 1)
    acc = None
    writes = []
    for b in range(rows // row_block):
        span = pl.ds(b * row_block, row_block)
        q = q_ref[span, :]
        go = go_ref[span, :]
        at = col + b * row_block
        spread = jnp.where((at >= owner * heads) & (at < (owner + 1) * heads), 1.0, 0.0)
        qdoc = lax.dot_general(
            blocks[0][:, width:], spread.astype(BF16), tn, preferred_element_type=F32
        )[:1]
        scores = lax.dot_general(keys, q, nt, preferred_element_type=F32) * scale
        scores = jnp.where(keydoc == qdoc, scores, -1e30)
        top = jnp.max(scores, axis=0, keepdims=True)
        probs = jnp.exp(scores - top)
        total = jnp.sum(probs, axis=0, keepdims=True)
        probs = probs * (1.0 / total)
        pgrad = lax.dot_general(keys, go, nt, preferred_element_type=F32)
        delta = jnp.sum(probs * pgrad, axis=0, keepdims=True)
        sgrad = (probs * (pgrad - delta)).astype(BF16)
        probs = probs.astype(BF16)
        dq[span, :] = (
            lax.dot_general(sgrad, keys, tn, preferred_element_type=F32) * scale
        ).astype(BF16)
        write = pltpu.make_async_copy(dq.at[span, :], dq_hbm.at[span, :], dq_sems.at[b])
        write.start()
        writes.append(write)
        term = jnp.dot(sgrad, q, preferred_element_type=F32) * scale
        term = term + jnp.dot(probs, go, preferred_element_type=F32)
        acc = term if acc is None else acc + term
    half = even_ref.shape[0]
    even_ref[...] = acc[:half, :].astype(BF16)
    odd_ref[...] = acc[half:, :].astype(BF16)
    for copy in writes + fetches:
        copy.wait()


def attention(queries, grad_out, blocks, weights):
    n_ctx = len(blocks)
    q_rows, heads, width = queries.shape
    rows = q_rows * heads
    keys = blocks[0].shape[0] * n_ctx
    row_block = min(256, rows)
    q = queries.reshape(rows, width)
    go = grad_out.reshape(rows, width)
    half = (keys // 2, width)
    outs = [
        jax.ShapeDtypeStruct((rows, width), BF16),
        jax.ShapeDtypeStruct(half, BF16),
        jax.ShapeDtypeStruct(half, BF16),
    ]
    outs += [pltpu.VMEM(w.shape[1:], BF16) for w in weights]
    res = call(
        functools.partial(attention_body, n_ctx, heads, row_block),
        outs,
        (q, go, *blocks, *weights),
        [vmem_spec()] * (2 + n_ctx) + [hbm_spec()] * 3,
        [
            pltpu.VMEM((keys, width), BF16),
            pltpu.VMEM((rows, width), BF16),
            pltpu.SemaphoreType.DMA((rows // row_block,)),
            pltpu.SemaphoreType.DMA((3,)),
        ],
        24 * MIB,
        flops=10 * rows * keys * width,
        out_specs=[hbm_spec()] + [vmem_spec()] * 5,
    )
    return res[0].reshape(queries.shape), res[1], res[2], res[3:]


def split_score(total, lane):
    high = total.astype(BF16).astype(F32)
    low = total - high
    return jnp.where(lane == 0, high, jnp.where(lane == 1, low, 0.0)).astype(BF16)


def expert_body(n_ctx, chunks, *refs):
    blocks = refs[:n_ctx]
    wg, wu, wd, even_ref, odd_ref, xt, xg = refs[n_ctx:]
    width, hid = wg.shape
    step = width // chunks
    per = blocks[0].shape[0] // 2
    for i, block in enumerate(blocks):
        xt[i * per : (i + 1) * per, :] = block[:per, :]
        xg[i * per : (i + 1) * per, :] = block[per:, :]
    rows = per * n_ctx
    nt = (((1,), (1,)), ((), ()))
    gate = jnp.zeros((rows, hid), F32)
    up = jnp.zeros((rows, hid), F32)
    act = jnp.zeros((rows, hid), F32)
    for c in range(chunks):
        cols = pl.ds(c * step, step)
        gate = gate + jnp.dot(xt[:, cols], wg[cols, :], preferred_element_type=F32)
        up = up + jnp.dot(xt[:, cols], wu[cols, :], preferred_element_type=F32)
        act = act + lax.dot_general(xg[:, cols], wd[:, cols], nt, preferred_element_type=F32)
    sig = jax.nn.sigmoid(gate)
    silu = gate * sig
    hidden = (silu * up).astype(BF16).astype(F32)
    score = jnp.sum(hidden * act, axis=1, keepdims=True)
    ggrad = (act * up * sig * (1.0 + gate * (1.0 - sig))).astype(BF16)
    ugrad = (act * silu).astype(BF16)
    half = rows // 2
    lane = lax.broadcasted_iota(jnp.int32, (rows, LANES), 1)
    tail = split_score(score, lane)
    even_ref[:, pl.ds(width, LANES)] = tail[:half]
    odd_ref[:, pl.ds(width, LANES)] = tail[half:]
    fine = 512
    for c in range(width // fine):
        cols = pl.ds(c * fine, fine)
        part = lax.dot_general(ggrad, wg[cols, :], nt, preferred_element_type=F32)
        part = part + lax.dot_general(ugrad, wu[cols, :], nt, preferred_element_type=F32)
        part = part.astype(BF16)
        even_ref[:, cols] = part[:half]
        odd_ref[:, cols] = part[half:]


def experts(blocks, weights):
    n_ctx = len(blocks)
    width = blocks[0].shape[1]
    hid = weights[0].shape[1]
    rows = blocks[0].shape[0] // 2 * n_ctx
    out = jax.ShapeDtypeStruct((rows // 2, width + LANES), BF16)
    weights = [pltpu.with_memory_space_constraint(w, pltpu.VMEM) for w in weights]
    return call(
        functools.partial(expert_body, n_ctx, 4),
        [out, out],
        (*blocks, *weights),
        [vmem_spec()] * (n_ctx + 3),
        [pltpu.VMEM((rows, width), BF16), pltpu.VMEM((rows, width), BF16)],
        min(30 * MIB, 4 * MIB + 6 * nbytes((rows, width), BF16)),
        flops=10 * rows * width * hid,
    )


def pair_body(n_out, keep_ref, got_ref, *outs):
    width = outs[0].shape[1] - LANES
    per = outs[0].shape[0]
    for i in range(n_out):
        span = pl.ds(i * per, per)
        total = keep_ref[span, :].astype(F32) + got_ref[span, :].astype(F32)
        outs[i][:, :width] = total[:, :width].astype(BF16)
        lane = lax.broadcasted_iota(jnp.int32, (per, LANES), 1)
        score = jnp.sum(total[:, width:], axis=1, keepdims=True)
        outs[i][:, pl.ds(width, LANES)] = split_score(score, lane)


def pair_sum(keep, got, n_out):
    rows, width = keep.shape
    outs = [jax.ShapeDtypeStruct((rows // n_out, width), BF16) for _ in range(n_out)]
    return call(
        functools.partial(pair_body, n_out),
        outs,
        (keep, got),
        [vmem_spec()] * 2,
        [],
        4 * MIB + 6 * nbytes(keep.shape, BF16),
    )


def owner_body(n_in, *refs):
    ins = refs[:n_in]
    outs = refs[n_in:]
    width = ins[0].shape[1] - LANES
    total = ins[0][...].astype(F32)
    for ref in ins[1:]:
        total = total + ref[...].astype(F32)
    score = jnp.sum(total[:, width:], axis=1, keepdims=True)
    lane = lax.broadcasted_iota(jnp.int32, (ins[0].shape[0], LANES), 1)
    tail = jnp.where(lane == 0, score, 0.0)
    for k, out in enumerate(outs):
        span = slice(k * CAP, (k + 1) * CAP)
        out[:, :width] = total[span, :width].astype(BF16)
        out[:, pl.ds(width, LANES)] = tail[span].astype(BF16)


def owner_sum(parts, n_out):
    rows, width = parts[0].shape
    outs = [jax.ShapeDtypeStruct((rows // n_out, width), BF16) for _ in range(n_out)]
    return call(
        functools.partial(owner_body, len(parts)),
        outs,
        tuple(parts),
        [vmem_spec()] * len(parts),
        [],
        4 * MIB + 8 * nbytes(parts[0].shape, F32),
    )


def final_body(n_exp, chunks, *refs):
    msgs = refs[:n_exp]
    weight_ref, chosen_ref, ids_ref, dtok_hbm, dgate_ref, out, sems = refs[n_exp:]
    width = msgs[0].shape[1] - LANES
    top, rows = ids_ref.shape
    slots = n_exp * CAP
    weight = weight_ref[...]
    high = weight.astype(BF16)
    rest = weight - high.astype(F32)
    mid = rest.astype(BF16)
    low = (rest - mid.astype(F32)).astype(BF16)
    lhs = jnp.concatenate([high, mid, low], axis=0)
    tn = (((0,), (0,)), ((), ()))
    step = width // chunks
    writes = []
    for c in range(chunks):
        cols = pl.ds(c * step, step)
        piece = jnp.concatenate([msg[:, cols] for msg in msgs], axis=0)
        stacked = jnp.concatenate([piece] * 3, axis=0)
        out[:, cols] = lax.dot_general(lhs, stacked, tn, preferred_element_type=F32).astype(BF16)
        write = pltpu.make_async_copy(out.at[:, cols], dtok_hbm.at[:, cols], sems.at[c])
        write.start()
        writes.append(write)
    tail = jnp.concatenate([msg[:, pl.ds(width, LANES)] for msg in msgs], axis=0)
    kept = chosen_ref[...] * tail[:, :1].astype(F32)
    expert = slot_experts((slots, rows))
    ids = ids_ref[...]
    grads = [
        jnp.sum(jnp.where(ids[j : j + 1] == expert, kept, 0.0), axis=0, keepdims=True)
        for j in range(top)
    ]
    dgate_ref[...] = jnp.concatenate(grads, axis=0).astype(BF16)
    for write in writes:
        write.wait()


def final(msgs, weight, chosen, expert_ids):
    n_exp = len(msgs)
    width = msgs[0].shape[1] - LANES
    rows, top = expert_ids.shape
    chunks = 4
    d_tokens, d_gates = call(
        functools.partial(final_body, n_exp, chunks),
        [
            jax.ShapeDtypeStruct((rows, width), BF16),
            jax.ShapeDtypeStruct((top, rows), BF16),
        ],
        (*msgs, weight, chosen, expert_ids.T),
        [vmem_spec()] * (n_exp + 3),
        [pltpu.VMEM((rows, width), BF16), pltpu.SemaphoreType.DMA((chunks,))],
        12 * MIB,
        flops=6 * n_exp * CAP * rows * width,
        out_specs=[hbm_spec(), vmem_spec()],
    )
    return d_tokens, d_gates.T


def gather_blocks(own, n_ctx):
    chips = n_ctx // 2
    line = [own] + [chip_exchange(own, p) for p in range(1, chips)]
    return line + [core_exchange(block) for block in line]


def widen_add(*arrays):
    total = arrays[0].astype(F32)
    for array in arrays[1:]:
        total = total + array.astype(F32)
    return total.astype(BF16)


def local(
    queries,
    latent,
    grad_out,
    doc_ids,
    tokens,
    token_grads,
    gate_values,
    expert_ids,
    gate_order,
    w_gate,
    w_up,
    w_down,
):
    n_ctx = lax.axis_size("ctx")
    n_exp = lax.axis_size("exp")
    assert w_gate.shape[0] == 1
    per_dev = latent.shape[0]

    chips = n_ctx // 2
    sends, weight, chosen = route(
        expert_ids, gate_order, gate_values, tokens, token_grads, n_exp
    )
    got = [sends[0]] + [exchange(sends[k], "exp", k) for k in range(1, n_exp)]
    own_rows = jnp.concatenate([g[:CAP] for g in got] + [g[CAP:] for g in got], axis=0)

    doc_cols = jnp.broadcast_to(doc_ids.astype(BF16)[:, None], (per_dev, LANES))
    lat_blocks = gather_blocks(jnp.concatenate([latent, doc_cols], axis=1), n_ctx)
    row_blocks = gather_blocks(own_rows, n_ctx)

    d_queries, lat_even, lat_odd, weights = attention(
        queries, grad_out, lat_blocks, (w_gate, w_up, w_down)
    )
    lat_sum = widen_add(lat_even, core_exchange(lat_odd))
    lat_parts = [lat_sum[:per_dev]]
    for p in range(1, chips):
        part = lat_sum[p * per_dev : (p + 1) * per_dev]
        lat_parts.append(chip_exchange(part, p))
    lat_total = widen_add(*lat_parts)
    mask = 1
    while mask < n_exp:
        lat_total = widen_add(lat_total, exchange(lat_total, "exp", mask))
        mask *= 2

    even, odd = experts(row_blocks, weights)
    summed = pair_sum(even, core_exchange(odd), chips)
    parts = [summed[0]] + [chip_exchange(summed[p], p) for p in range(1, chips)]
    backs = owner_sum(parts, n_exp)
    back = [backs[0]] + [exchange(backs[k], "exp", k) for k in range(1, n_exp)]
    d_tokens, d_gates = final(back, weight, chosen, expert_ids)
    return (d_queries, lat_total, d_tokens, d_gates)


def solution(mesh):
    in_specs = (
        P("ctx", "exp", None),
        P("ctx", None),
        P("ctx", "exp", None),
        P("ctx"),
        P(("ctx", "exp"), None),
        P(("ctx", "exp"), None),
        P(("ctx", "exp"), None),
        P(("ctx", "exp"), None),
        P(("ctx", "exp"), None),
        P("exp", None, "ctx"),
        P("exp", None, "ctx"),
        P("exp", "ctx", None),
    )
    out_specs = (
        P("ctx", "exp", None),
        P("ctx", None),
        P(("ctx", "exp"), None),
        P(("ctx", "exp"), None),
    )
    return jax.shard_map(local, mesh=mesh, in_specs=in_specs, out_specs=out_specs, check_vma=False)
```

profile of v0, /device:TPU:0, one launch (start us, length us, event | category | flops | bytes accessed | tf_op | source)
XLA Modules:
  0.0 92.2 jit_solution(9633645342692355074)
XLA Ops:
  0.7 0.8 convert_element_type.45
  1.5 0.1 broadcast_in_dim.2
  1.5 0.9 pad_maximum_fusion.refs_2_
  2.4 3.0 %collective-permute-start = (bf16[64,640]{1,0:T(8,128)(2,1)S(1)}, bf16[64,640]{1,0:T(8,128)(2,1)S(1)}, u32[]{:S(2)}, u32[]{:S(2)}) collective-permute-start(bf16[64,640]{1,0:T(8,128)(2,1)S(1)} %pad_maximum_fusion.refs_2_), channel_id=1, source_target_pairs={{0,8},{4,20},{8,0},{12,28},{16,24},{20,4},{24,16},{28,12},{1,9},{5... | collective-permute-start | bytes 245768 | tf_op jit(solution)/shard_map/ppermute | solution.py:31
  5.4 1.5 %collective-permute-start.1 = (bf16[64,640]{1,0:T(8,128)(2,1)S(1)}, bf16[64,640]{1,0:T(8,128)(2,1)S(1)}, u32[]{:S(2)}, u32[]{:S(2)}) collective-permute-start(bf16[64,640]{1,0:T(8,128)(2,1)S(1)} %pad_maximum_fusion.refs_2_), channel_id=1, source_target_pairs={{0,16},{4,12},{8,24},{12,4},{16,0},{20,28},{24,8},{28,20},{1,17},{... | collective-permute-start | bytes 245768 | tf_op jit(solution)/shard_map/ppermute | solution.py:31
  6.9 0.0 collective-permute-start.2
  6.9 0.0 collective-permute-start.3
  6.9 2.5 %shard_map.148 = (bf16[4,7168]{1,0:T(4,128)(2,1)S(1)}, bf16[4,7168]{1,0:T(4,128)(2,1)S(1)}, bf16[4,7168]{1,0:T(4,128)(2,1)S(1)}, bf16[4,7168]{1,0:T(4,128)(2,1)S...) custom-call(s32[8,128]{1,0:T(8,128)} %bitcast.8, s32[1,128]{1,0:T(1,128)} %order_hbm.1, f32[8,128]{1,0:T(8,128)} %bitcast.10, ...), custom_call_target="tpu_custom_call" | custom-call | flops 29360128 | bytes 3916288 | tf_op jit(solution)/shard_map/pallas_call | solution.py:60
  9.4 2.1 %collective-permute-start.13 = (bf16[4,7168]{1,0:T(4,128)(2,1)S(1)}, bf16[4,7168]{1,0:T(4,128)(2,1)S(1)}, u32[]{:S(2)}, u32[]{:S(2)}) collective-permute-start(bf16[4,7168]{1,0:T(4,128)(2,1)S(1)} %get-tuple-element.32), channel_id=1, source_target_pairs={{0,1},{1,0},{2,3},{3,2},{4,5},{5,4},{6,7},{7,6},{8,9},{9,8},{10,11... | collective-permute-start | bytes 172040 | tf_op jit(solution)/shard_map/ppermute | solution.py:21
  11.5 2.5 %collective-permute-done.13 = bf16[4,7168]{1,0:T(4,128)(2,1)S(1)} collective-permute-done((bf16[4,7168]{1,0:T(4,128)(2,1)S(1)}, bf16[4,7168]{1,0:T(4,128)(2,1)S(1)}, u32[]{:S(2)}, u32[]{:S(2)}) %collective-permute-start.13) | collective-permute-done | bytes 57376 | tf_op jit(solution)/shard_map/ppermute | solution.py:21
  14.1 2.8 %collective-permute-start.14 = (bf16[4,7168]{1,0:T(4,128)(2,1)S(1)}, bf16[4,7168]{1,0:T(4,128)(2,1)S(1)}, u32[]{:S(2)}, u32[]{:S(2)}) collective-permute-start(bf16[4,7168]{1,0:T(4,128)(2,1)S(1)} %get-tuple-element.33), channel_id=1, source_target_pairs={{0,2},{1,3},{2,0},{3,1},{4,6},{5,7},{6,4},{7,5},{8,10},{9,11},{10,... | collective-permute-start | bytes 172040 | tf_op jit(solution)/shard_map/ppermute | solution.py:21
  16.9 2.7 %collective-permute-done.14 = bf16[4,7168]{1,0:T(4,128)(2,1)S(1)} collective-permute-done((bf16[4,7168]{1,0:T(4,128)(2,1)S(1)}, bf16[4,7168]{1,0:T(4,128)(2,1)S(1)}, u32[]{:S(2)}, u32[]{:S(2)}) %collective-permute-start.14) | collective-permute-done | bytes 57376 | tf_op jit(solution)/shard_map/ppermute | solution.py:21
  19.6 3.8 %collective-permute-start.15 = (bf16[4,7168]{1,0:T(4,128)(2,1)S(1)}, bf16[4,7168]{1,0:T(4,128)(2,1)S(1)}, u32[]{:S(2)}, u32[]{:S(2)}) collective-permute-start(bf16[4,7168]{1,0:T(4,128)(2,1)S(1)} %get-tuple-element.34), channel_id=1, source_target_pairs={{0,3},{1,2},{2,1},{3,0},{4,7},{5,6},{6,5},{7,4},{8,11},{9,10},{10,... | collective-permute-start | bytes 172040 | tf_op jit(solution)/shard_map/ppermute | solution.py:21
  23.4 0.5 collective-permute-start.5
  23.9 0.1 collective-permute-start.6
  24.1 0.0 collective-permute-done.3.refs_6_
  24.1 0.6 collective-permute-done.4.refs_7_
  24.7 0.2 collective-permute-done.5.refs_8_
  24.9 0.4 collective-permute-done.6.refs_9_
  25.2 6.9 %shard_map.147 = (bf16[1024,512]{1,0:T(8,128)(2,1)}, bf16[256,512]{1,0:T(8,128)(2,1)S(1)}, bf16[256,512]{1,0:T(8,128)(2,1)S(1)}, bf16[7168,256]{1,0:T(8,128)(2,1...) custom-call(bf16[1024,512]{1,0:T(8,128)(2,1)S(1)} %bitcast.6, bf16[1024,512]{1,0:T(8,128)(2,1)S(1)} %bitcast.7, ...), custom_call_target="tpu_custom_call" | custom-call | flops 2684354560 | bytes 26345472 | tf_op jit(solution)/shard_map/pallas_call | solution.py:60
  32.2 1.8 %copy-done = bf16[7168,256]{1,0:T(8,128)(2,1)} copy-done((bf16[7168,256]{1,0:T(8,128)(2,1)}, bf16[7168,256]{1,0:T(8,128)(2,1)S(1)}, u32[]{:S(2)}) %copy-start) | copy-done | bytes 3670040
  34.0 1.8 %copy-done.2 = bf16[7168,256]{1,0:T(8,128)(2,1)} copy-done((bf16[7168,256]{1,0:T(8,128)(2,1)}, bf16[7168,256]{1,0:T(8,128)(2,1)S(1)}, u32[]{:S(2)}) %copy-start.2) | copy-done | bytes 3670040
  35.7 1.9 %copy-done.4 = bf16[256,7168]{1,0:T(8,128)(2,1)} copy-done((bf16[256,7168]{1,0:T(8,128)(2,1)}, bf16[256,7168]{1,0:T(8,128)(2,1)S(1)}, u32[]{:S(2)}) %copy-start.4) | copy-done | bytes 3670040
  37.6 0.2 collective-permute-start.7
  37.8 0.3 concatenate.7.refs_0_
  38.2 1.6 %collective-permute-start.16 = (bf16[16,7168]{1,0:T(8,128)(2,1)S(1)}, bf16[16,7168]{1,0:T(8,128)(2,1)S(1)}, u32[]{:S(2)}, u32[]{:S(2)}) collective-permute-start(bf16[16,7168]{1,0:T(8,128)(2,1)S(1)} %concatenate.7.refs_0_), channel_id=1, source_target_pairs={{0,8},{4,20},{8,0},{12,28},{16,24},{20,4},{24,16},{28,12},{1,9},{5... | collective-permute-start | bytes 688136 | tf_op jit(solution)/shard_map/ppermute | solution.py:31
  39.8 1.5 %collective-permute-start.17 = (bf16[16,7168]{1,0:T(8,128)(2,1)S(1)}, bf16[16,7168]{1,0:T(8,128)(2,1)S(1)}, u32[]{:S(2)}, u32[]{:S(2)}) collective-permute-start(bf16[16,7168]{1,0:T(8,128)(2,1)S(1)} %concatenate.7.refs_0_), channel_id=1, source_target_pairs={{0,16},{4,12},{8,24},{12,4},{16,0},{20,28},{24,8},{28,20},{1,17},{... | collective-permute-start | bytes 688136 | tf_op jit(solution)/shard_map/ppermute | solution.py:31
  41.3 0.5 collective-permute-start.18
  41.8 0.0 collective-permute-start.19
  41.8 4.3 %collective-permute-done.16.refs_1_ = bf16[16,7168]{1,0:T(8,128)(2,1)S(1)} collective-permute-done((bf16[16,7168]{1,0:T(8,128)(2,1)S(1)}, bf16[16,7168]{1,0:T(8,128)(2,1)S(1)}, u32[]{:S(2)}, u32[]{:S(2)}) %collective-permute-start.16) | collective-permute-done | bytes 229408 | tf_op jit(solution)/shard_map/ppermute | solution.py:31
  46.1 0.0 collective-permute-start.20
  46.1 0.0 collective-permute-done.17.refs_2_
  46.1 1.1 %collective-permute-start.21 = (bf16[16,7168]{1,0:T(8,128)(2,1)S(1)}, bf16[16,7168]{1,0:T(8,128)(2,1)S(1)}, u32[]{:S(2)}, u32[]{:S(2)}) collective-permute-start(bf16[16,7168]{1,0:T(8,128)(2,1)S(1)} %collective-permute-done.17.refs_2_), channel_id=1, source_target_pairs={{0,4},{4,0},{8,12},{12,8},{16,20},{20,16},{24,28},{28,24},{1,5},{5... | collective-permute-start | bytes 688136 | tf_op jit(solution)/shard_map/ppermute | solution.py:21
  47.2 5.0 %collective-permute-done.18.refs_3_ = bf16[16,7168]{1,0:T(8,128)(2,1)S(1)} collective-permute-done((bf16[16,7168]{1,0:T(8,128)(2,1)S(1)}, bf16[16,7168]{1,0:T(8,128)(2,1)S(1)}, u32[]{:S(2)}, u32[]{:S(2)}) %collective-permute-start.18) | collective-permute-done | bytes 229408 | tf_op jit(solution)/shard_map/ppermute | solution.py:31
  52.2 0.1 add_convert_fusion
  52.3 1.4 %collective-permute-done.22.refs_7_ = bf16[16,7168]{1,0:T(8,128)(2,1)S(1)} collective-permute-done((bf16[16,7168]{1,0:T(8,128)(2,1)S(1)}, bf16[16,7168]{1,0:T(8,128)(2,1)S(1)}, u32[]{:S(2)}, u32[]{:S(2)}) %collective-permute-start.22) | collective-permute-done | bytes 229408 | tf_op jit(solution)/shard_map/ppermute | solution.py:21
  53.7 2.0 %copy-done.1 = bf16[7168,256]{1,0:T(8,128)(2,1)S(1)} copy-done((bf16[7168,256]{1,0:T(8,128)(2,1)S(1)}, bf16[7168,256]{1,0:T(8,128)(2,1)}, u32[]{:S(2)}) %copy-start.1) | copy-done | bytes 3670040
  55.8 2.0 %copy-done.3 = bf16[7168,256]{1,0:T(8,128)(2,1)S(1)} copy-done((bf16[7168,256]{1,0:T(8,128)(2,1)S(1)}, bf16[7168,256]{1,0:T(8,128)(2,1)}, u32[]{:S(2)}) %copy-start.3) | copy-done | bytes 3670040
  57.8 2.0 %copy-done.5 = bf16[256,7168]{1,0:T(8,128)(2,1)S(1)} copy-done((bf16[256,7168]{1,0:T(8,128)(2,1)S(1)}, bf16[256,7168]{1,0:T(8,128)(2,1)}, u32[]{:S(2)}) %copy-start.5) | copy-done | bytes 3670040
  59.8 6.2 %shard_map.149 = (bf16[32,7296]{1,0:T(8,128)(2,1)S(1)}, bf16[32,7296]{1,0:T(8,128)(2,1)S(1)}) custom-call(bf16[16,7168]{1,0:T(8,128)(2,1)S(1)} %concatenate.7.refs_0_, bf16[16,7168]{1,0:T(8,128)(2,1)S(1)} %collective-permute-done.16.refs_1_, bf16[16,7168]{1,0:T(8,128)(2,1)S(1)} %collective-permute-done.17.refs_2_, ...), custom_call_target="tpu_custom_call" | custom-call | flops 1174405120 | bytes 13778944 | tf_op jit(solution)/shard_map/pallas_call | solution.py:60
  66.0 0.2 collective-permute-start.23
  66.2 1.6 %collective-permute-start.10 = (bf16[64,512]{1,0:T(8,128)(2,1)S(1)}, bf16[64,512]{1,0:T(8,128)(2,1)S(1)}, u32[]{:S(2)}, u32[]{:S(2)}) collective-permute-start(bf16[64,512]{1,0:T(8,128)(2,1)S(1)} %get-tuple-element.53), channel_id=1, source_target_pairs={{0,24},{4,28},{8,16},{12,20},{16,8},{20,12},{24,0},{28,4},{1,25},{... | collective-permute-start | bytes 196616 | tf_op jit(solution)/shard_map/ppermute | solution.py:31
  67.8 1.4 %collective-permute-start.9 = (bf16[64,512]{1,0:T(8,128)(2,1)S(1)}, bf16[64,512]{1,0:T(8,128)(2,1)S(1)}, u32[]{:S(2)}, u32[]{:S(2)}) collective-permute-start(bf16[64,512]{1,0:T(8,128)(2,1)S(1)} %get-tuple-element.54), channel_id=1, source_target_pairs={{0,16},{4,12},{8,24},{12,4},{16,0},{20,28},{24,8},{28,20},{1,17},{... | collective-permute-start | bytes 196616 | tf_op jit(solution)/shard_map/ppermute | solution.py:31
  69.3 0.5 collective-permute-start.8
  69.8 2.0 %collective-permute-done.10 = bf16[64,512]{1,0:T(8,128)(2,1)S(1)} collective-permute-done((bf16[64,512]{1,0:T(8,128)(2,1)S(1)}, bf16[64,512]{1,0:T(8,128)(2,1)S(1)}, u32[]{:S(2)}, u32[]{:S(2)}) %collective-permute-start.10) | collective-permute-done | bytes 65568 | tf_op jit(solution)/shard_map/ppermute | solution.py:31
  71.8 1.2 %collective-permute-done.9 = bf16[64,512]{1,0:T(8,128)(2,1)S(1)} collective-permute-done((bf16[64,512]{1,0:T(8,128)(2,1)S(1)}, bf16[64,512]{1,0:T(8,128)(2,1)S(1)}, u32[]{:S(2)}, u32[]{:S(2)}) %collective-permute-start.9) | collective-permute-done | bytes 65568 | tf_op jit(solution)/shard_map/ppermute | solution.py:31
  73.0 0.5 collective-permute-done.8
  73.6 0.1 collective-permute-start.11
  73.7 0.2 shard_map.150
  73.8 1.0 %collective-permute-start.24 = (bf16[8,7296]{1,0:T(8,128)(2,1)S(1)}, bf16[8,7296]{1,0:T(8,128)(2,1)S(1)}, u32[]{:S(2)}, u32[]{:S(2)}) collective-permute-start(bf16[8,7296]{1,0:T(8,128)(2,1)S(1)} %get-tuple-element.41), channel_id=1, source_target_pairs={{0,8},{4,20},{8,0},{12,28},{16,24},{20,4},{24,16},{28,12},{1,9},{5... | collective-permute-start | bytes 350216 | tf_op jit(solution)/shard_map/ppermute | solution.py:31
  74.8 0.6 collective-permute-start.25
  75.4 2.0 %collective-permute-start.26 = (bf16[8,7296]{1,0:T(8,128)(2,1)S(1)}, bf16[8,7296]{1,0:T(8,128)(2,1)S(1)}, u32[]{:S(2)}, u32[]{:S(2)}) collective-permute-start(bf16[8,7296]{1,0:T(8,128)(2,1)S(1)} %get-tuple-element.43), channel_id=1, source_target_pairs={{0,24},{4,28},{8,16},{12,20},{16,8},{20,12},{24,0},{28,4},{1,25},{... | collective-permute-start | bytes 350216 | tf_op jit(solution)/shard_map/ppermute | solution.py:31
  77.4 0.5 collective-permute-done.11
  77.9 0.1 collective-permute-start.12
  78.0 0.9 %collective-permute-done.24.refs_1_ = bf16[8,7296]{1,0:T(8,128)(2,1)S(1)} collective-permute-done((bf16[8,7296]{1,0:T(8,128)(2,1)S(1)}, bf16[8,7296]{1,0:T(8,128)(2,1)S(1)}, u32[]{:S(2)}, u32[]{:S(2)}) %collective-permute-start.24) | collective-permute-done | bytes 116768 | tf_op jit(solution)/shard_map/ppermute | solution.py:31
  79.0 1.0 %collective-permute-done.25.refs_2_ = bf16[8,7296]{1,0:T(8,128)(2,1)S(1)} collective-permute-done((bf16[8,7296]{1,0:T(8,128)(2,1)S(1)}, bf16[8,7296]{1,0:T(8,128)(2,1)S(1)}, u32[]{:S(2)}, u32[]{:S(2)}) %collective-permute-start.25) | collective-permute-done | bytes 116768 | tf_op jit(solution)/shard_map/ppermute | solution.py:31
  79.9 2.2 %collective-permute-done.26.refs_3_ = bf16[8,7296]{1,0:T(8,128)(2,1)S(1)} collective-permute-done((bf16[8,7296]{1,0:T(8,128)(2,1)S(1)}, bf16[8,7296]{1,0:T(8,128)(2,1)S(1)}, u32[]{:S(2)}, u32[]{:S(2)}) %collective-permute-start.26) | collective-permute-done | bytes 116768 | tf_op jit(solution)/shard_map/ppermute | solution.py:31
  82.2 0.1 shard_map.151
  82.3 2.0 %collective-permute-start.27 = (bf16[2,7296]{1,0:T(2,128)(2,1)S(1)}, bf16[2,7296]{1,0:T(2,128)(2,1)S(1)}, u32[]{:S(2)}, u32[]{:S(2)}) collective-permute-start(bf16[2,7296]{1,0:T(2,128)(2,1)S(1)} %get-tuple-element.45), channel_id=1, source_target_pairs={{0,1},{1,0},{2,3},{3,2},{4,5},{5,4},{6,7},{7,6},{8,9},{9,8},{10,11... | collective-permute-start | bytes 87560 | tf_op jit(solution)/shard_map/ppermute | solution.py:21
  84.3 2.4 %collective-permute-start.29 = (bf16[2,7296]{1,0:T(2,128)(2,1)S(1)}, bf16[2,7296]{1,0:T(2,128)(2,1)S(1)}, u32[]{:S(2)}, u32[]{:S(2)}) collective-permute-start(bf16[2,7296]{1,0:T(2,128)(2,1)S(1)} %get-tuple-element.47), channel_id=1, source_target_pairs={{0,3},{1,2},{2,1},{3,0},{4,7},{5,6},{6,5},{7,4},{8,11},{9,10},{10,... | collective-permute-start | bytes 87560 | tf_op jit(solution)/shard_map/ppermute | solution.py:21
  86.8 0.6 add_convert_fusion.1
  87.4 1.7 %collective-permute-done.28.refs_2_ = bf16[2,7296]{1,0:T(2,128)(2,1)S(1)} collective-permute-done((bf16[2,7296]{1,0:T(2,128)(2,1)S(1)}, bf16[2,7296]{1,0:T(2,128)(2,1)S(1)}, u32[]{:S(2)}, u32[]{:S(2)}) %collective-permute-start.28) | collective-permute-done | bytes 29216 | tf_op jit(solution)/shard_map/ppermute | solution.py:21
  89.1 0.9 collective-permute-done.29.refs_3_
  90.0 2.2 %shard_map.152 = (bf16[128,7168]{1,0:T(8,128)(2,1)}, bf16[8,128]{1,0:T(8,128)(2,1)}) custom-call(bf16[2,7296]{1,0:T(2,128)(2,1)S(1)} %get-tuple-element.44.refs_0_, bf16[2,7296]{1,0:T(2,128)(2,1)S(1)} %collective-permute-done.27.refs_1_, bf16[2,7296]{1,0:T(2,128)(2,1)S(1)} %collective-permute-done.28.refs_2_, ...), custom_call_target="tpu_custom_call" | custom-call | flops 44040192 | bytes 1966080 | tf_op jit(solution)/shard_map/pallas_call | solution.py:60
  (33 shorter events, 0.3 us)
Async XLA Ops:
  0.6 24.6 %copy-start.6 = (bf16[64,16,512]{2,1,0:T(8,128)(2,1)S(1)}, bf16[64,16,512]{2,1,0:T(8,128)(2,1)}, u32[]{:S(2)}) copy-start(bf16[64,16,512]{2,1,0:T(8,128)(2,1)} %param.12) | copy-start | bytes 3145732
  0.6 24.6 %copy-start.7 = (bf16[64,16,512]{2,1,0:T(8,128)(2,1)S(1)}, bf16[64,16,512]{2,1,0:T(8,128)(2,1)}, u32[]{:S(2)}) copy-start(bf16[64,16,512]{2,1,0:T(8,128)(2,1)} %param.14) | copy-start | bytes 3145732
  2.4 21.0 %collective-permute-start = (bf16[64,640]{1,0:T(8,128)(2,1)S(1)}, bf16[64,640]{1,0:T(8,128)(2,1)S(1)}, u32[]{:S(2)}, u32[]{:S(2)}) collective-permute-start(bf16[64,640]{1,0:T(8,128)(2,1)S(1)} %pad_maximum_fusion.refs_2_), channel_id=1, source_target_pairs={{0,8},{4,20},{8,0},{12,28},{16,24},{20,4},{24,16},{28,12},{1,9},{5... | collective-permute-start | bytes 245768 | tf_op jit(solution)/shard_map/ppermute | solution.py:31
  5.4 18.1 %collective-permute-start.1 = (bf16[64,640]{1,0:T(8,128)(2,1)S(1)}, bf16[64,640]{1,0:T(8,128)(2,1)S(1)}, u32[]{:S(2)}, u32[]{:S(2)}) collective-permute-start(bf16[64,640]{1,0:T(8,128)(2,1)S(1)} %pad_maximum_fusion.refs_2_), channel_id=1, source_target_pairs={{0,16},{4,12},{8,24},{12,4},{16,0},{20,28},{24,8},{28,20},{1,17},{... | collective-permute-start | bytes 245768 | tf_op jit(solution)/shard_map/ppermute | solution.py:31
  6.9 17.1 %collective-permute-start.2 = (bf16[64,640]{1,0:T(8,128)(2,1)S(1)}, bf16[64,640]{1,0:T(8,128)(2,1)S(1)}, u32[]{:S(2)}, u32[]{:S(2)}) collective-permute-start(bf16[64,640]{1,0:T(8,128)(2,1)S(1)} %pad_maximum_fusion.refs_2_), channel_id=1, source_target_pairs={{0,24},{4,28},{8,16},{12,20},{16,8},{20,12},{24,0},{28,4},{1,25},{... | collective-permute-start | bytes 245768 | tf_op jit(solution)/shard_map/ppermute | solution.py:31
  6.9 17.2 %collective-permute-start.3 = (bf16[64,640]{1,0:T(8,128)(2,1)S(1)}, bf16[64,640]{1,0:T(8,128)(2,1)S(1)}, u32[]{:S(2)}, u32[]{:S(2)}) collective-permute-start(bf16[64,640]{1,0:T(8,128)(2,1)S(1)} %pad_maximum_fusion.refs_2_), channel_id=1, source_target_pairs={{0,4},{4,0},{8,12},{12,8},{16,20},{20,16},{24,28},{28,24},{1,5},{5... | collective-permute-start | bytes 245768 | tf_op jit(solution)/shard_map/ppermute | solution.py:21
  9.4 4.7 %collective-permute-start.13 = (bf16[4,7168]{1,0:T(4,128)(2,1)S(1)}, bf16[4,7168]{1,0:T(4,128)(2,1)S(1)}, u32[]{:S(2)}, u32[]{:S(2)}) collective-permute-start(bf16[4,7168]{1,0:T(4,128)(2,1)S(1)} %get-tuple-element.32), channel_id=1, source_target_pairs={{0,1},{1,0},{2,3},{3,2},{4,5},{5,4},{6,7},{7,6},{8,9},{9,8},{10,11... | collective-permute-start | bytes 172040 | tf_op jit(solution)/shard_map/ppermute | solution.py:21
  14.1 5.5 %collective-permute-start.14 = (bf16[4,7168]{1,0:T(4,128)(2,1)S(1)}, bf16[4,7168]{1,0:T(4,128)(2,1)S(1)}, u32[]{:S(2)}, u32[]{:S(2)}) collective-permute-start(bf16[4,7168]{1,0:T(4,128)(2,1)S(1)} %get-tuple-element.33), channel_id=1, source_target_pairs={{0,2},{1,3},{2,0},{3,1},{4,6},{5,7},{6,4},{7,5},{8,10},{9,11},{10,... | collective-permute-start | bytes 172040 | tf_op jit(solution)/shard_map/ppermute | solution.py:21
  19.6 18.2 %collective-permute-start.15 = (bf16[4,7168]{1,0:T(4,128)(2,1)S(1)}, bf16[4,7168]{1,0:T(4,128)(2,1)S(1)}, u32[]{:S(2)}, u32[]{:S(2)}) collective-permute-start(bf16[4,7168]{1,0:T(4,128)(2,1)S(1)} %get-tuple-element.34), channel_id=1, source_target_pairs={{0,3},{1,2},{2,1},{3,0},{4,7},{5,6},{6,5},{7,4},{8,11},{9,10},{10,... | collective-permute-start | bytes 172040 | tf_op jit(solution)/shard_map/ppermute | solution.py:21
  23.4 1.3 %collective-permute-start.4 = (bf16[64,640]{1,0:T(8,128)(2,1)S(1)}, bf16[64,640]{1,0:T(8,128)(2,1)S(1)}, u32[]{:S(2)}, u32[]{:S(2)}) collective-permute-start(bf16[64,640]{1,0:T(8,128)(2,1)S(1)} %collective-permute-done.refs_3_), channel_id=1, source_target_pairs={{0,4},{4,0},{8,12},{12,8},{16,20},{20,16},{24,28},{28,24},{1,5},{5... | collective-permute-start | bytes 245768 | tf_op jit(solution)/shard_map/ppermute | solution.py:21
  23.4 1.4 %collective-permute-start.5 = (bf16[64,640]{1,0:T(8,128)(2,1)S(1)}, bf16[64,640]{1,0:T(8,128)(2,1)S(1)}, u32[]{:S(2)}, u32[]{:S(2)}) collective-permute-start(bf16[64,640]{1,0:T(8,128)(2,1)S(1)} %collective-permute-done.1.refs_4_), channel_id=1, source_target_pairs={{0,4},{4,0},{8,12},{12,8},{16,20},{20,16},{24,28},{28,24},{1,5},{5... | collective-permute-start | bytes 245768 | tf_op jit(solution)/shard_map/ppermute | solution.py:21
  23.9 1.3 %collective-permute-start.6 = (bf16[64,640]{1,0:T(8,128)(2,1)S(1)}, bf16[64,640]{1,0:T(8,128)(2,1)S(1)}, u32[]{:S(2)}, u32[]{:S(2)}) collective-permute-start(bf16[64,640]{1,0:T(8,128)(2,1)S(1)} %collective-permute-done.2.refs_5_), channel_id=1, source_target_pairs={{0,4},{4,0},{8,12},{12,8},{16,20},{20,16},{24,28},{28,24},{1,5},{5... | collective-permute-start | bytes 245768 | tf_op jit(solution)/shard_map/ppermute | solution.py:21
  32.1 1.8 %copy-start = (bf16[7168,256]{1,0:T(8,128)(2,1)}, bf16[7168,256]{1,0:T(8,128)(2,1)S(1)}, u32[]{:S(2)}) copy-start(bf16[7168,256]{1,0:T(8,128)(2,1)S(1)} %get-tuple-element.35.refs_8_) | copy-start | bytes 11010052
  34.0 1.8 %copy-start.2 = (bf16[7168,256]{1,0:T(8,128)(2,1)}, bf16[7168,256]{1,0:T(8,128)(2,1)S(1)}, u32[]{:S(2)}) copy-start(bf16[7168,256]{1,0:T(8,128)(2,1)S(1)} %get-tuple-element.36.refs_9_) | copy-start | bytes 11010052
  35.7 1.9 %copy-start.4 = (bf16[256,7168]{1,0:T(8,128)(2,1)}, bf16[256,7168]{1,0:T(8,128)(2,1)S(1)}, u32[]{:S(2)}) copy-start(bf16[256,7168]{1,0:T(8,128)(2,1)S(1)} %get-tuple-element.37.refs_10_) | copy-start | bytes 11010052
  37.6 14.6 %collective-permute-start.7 = (bf16[256,512]{1,0:T(8,128)(2,1)S(1)}, bf16[256,512]{1,0:T(8,128)(2,1)S(1)}, u32[]{:S(2)}, u32[]{:S(2)}) collective-permute-start(bf16[256,512]{1,0:T(8,128)(2,1)S(1)} %get-tuple-element.30), channel_id=1, source_target_pairs={{0,4},{4,0},{8,12},{12,8},{16,20},{20,16},{24,28},{28,24},{1,5},{5... | collective-permute-start | bytes 786440 | tf_op jit(solution)/shard_map/ppermute | solution.py:21
  38.2 7.9 %collective-permute-start.16 = (bf16[16,7168]{1,0:T(8,128)(2,1)S(1)}, bf16[16,7168]{1,0:T(8,128)(2,1)S(1)}, u32[]{:S(2)}, u32[]{:S(2)}) collective-permute-start(bf16[16,7168]{1,0:T(8,128)(2,1)S(1)} %concatenate.7.refs_0_), channel_id=1, source_target_pairs={{0,8},{4,20},{8,0},{12,28},{16,24},{20,4},{24,16},{28,12},{1,9},{5... | collective-permute-start | bytes 688136 | tf_op jit(solution)/shard_map/ppermute | solution.py:31
  39.8 6.4 %collective-permute-start.17 = (bf16[16,7168]{1,0:T(8,128)(2,1)S(1)}, bf16[16,7168]{1,0:T(8,128)(2,1)S(1)}, u32[]{:S(2)}, u32[]{:S(2)}) collective-permute-start(bf16[16,7168]{1,0:T(8,128)(2,1)S(1)} %concatenate.7.refs_0_), channel_id=1, source_target_pairs={{0,16},{4,12},{8,24},{12,4},{16,0},{20,28},{24,8},{28,20},{1,17},{... | collective-permute-start | bytes 688136 | tf_op jit(solution)/shard_map/ppermute | solution.py:31
  41.3 11.0 %collective-permute-start.18 = (bf16[16,7168]{1,0:T(8,128)(2,1)S(1)}, bf16[16,7168]{1,0:T(8,128)(2,1)S(1)}, u32[]{:S(2)}, u32[]{:S(2)}) collective-permute-start(bf16[16,7168]{1,0:T(8,128)(2,1)S(1)} %concatenate.7.refs_0_), channel_id=1, source_target_pairs={{0,24},{4,28},{8,16},{12,20},{16,8},{20,12},{24,0},{28,4},{1,25},{... | collective-permute-start | bytes 688136 | tf_op jit(solution)/shard_map/ppermute | solution.py:31
  41.8 10.6 %collective-permute-start.19 = (bf16[16,7168]{1,0:T(8,128)(2,1)S(1)}, bf16[16,7168]{1,0:T(8,128)(2,1)S(1)}, u32[]{:S(2)}, u32[]{:S(2)}) collective-permute-start(bf16[16,7168]{1,0:T(8,128)(2,1)S(1)} %concatenate.7.refs_0_), channel_id=1, source_target_pairs={{0,4},{4,0},{8,12},{12,8},{16,20},{20,16},{24,28},{28,24},{1,5},{5... | collective-permute-start | bytes 688136 | tf_op jit(solution)/shard_map/ppermute | solution.py:21
  46.1 6.2 %collective-permute-start.20 = (bf16[16,7168]{1,0:T(8,128)(2,1)S(1)}, bf16[16,7168]{1,0:T(8,128)(2,1)S(1)}, u32[]{:S(2)}, u32[]{:S(2)}) collective-permute-start(bf16[16,7168]{1,0:T(8,128)(2,1)S(1)} %collective-permute-done.16.refs_1_), channel_id=1, source_target_pairs={{0,4},{4,0},{8,12},{12,8},{16,20},{20,16},{24,28},{28,24},{1,5},{5... | collective-permute-start | bytes 688136 | tf_op jit(solution)/shard_map/ppermute | solution.py:21
  46.1 6.2 %collective-permute-start.21 = (bf16[16,7168]{1,0:T(8,128)(2,1)S(1)}, bf16[16,7168]{1,0:T(8,128)(2,1)S(1)}, u32[]{:S(2)}, u32[]{:S(2)}) collective-permute-start(bf16[16,7168]{1,0:T(8,128)(2,1)S(1)} %collective-permute-done.17.refs_2_), channel_id=1, source_target_pairs={{0,4},{4,0},{8,12},{12,8},{16,20},{20,16},{24,28},{28,24},{1,5},{5... | collective-permute-start | bytes 688136 | tf_op jit(solution)/shard_map/ppermute | solution.py:21
  52.2 1.5 %collective-permute-start.22 = (bf16[16,7168]{1,0:T(8,128)(2,1)S(1)}, bf16[16,7168]{1,0:T(8,128)(2,1)S(1)}, u32[]{:S(2)}, u32[]{:S(2)}) collective-permute-start(bf16[16,7168]{1,0:T(8,128)(2,1)S(1)} %collective-permute-done.18.refs_3_), channel_id=1, source_target_pairs={{0,4},{4,0},{8,12},{12,8},{16,20},{20,16},{24,28},{28,24},{1,5},{5... | collective-permute-start | bytes 688136 | tf_op jit(solution)/shard_map/ppermute | solution.py:21
  53.7 2.0 %copy-start.1 = (bf16[7168,256]{1,0:T(8,128)(2,1)S(1)}, bf16[7168,256]{1,0:T(8,128)(2,1)}, u32[]{:S(2)}) copy-start(bf16[7168,256]{1,0:T(8,128)(2,1)} %copy-done) | copy-start | bytes 11010052
  55.8 2.0 %copy-start.3 = (bf16[7168,256]{1,0:T(8,128)(2,1)S(1)}, bf16[7168,256]{1,0:T(8,128)(2,1)}, u32[]{:S(2)}) copy-start(bf16[7168,256]{1,0:T(8,128)(2,1)} %copy-done.2) | copy-start | bytes 11010052
  57.8 2.0 %copy-start.5 = (bf16[256,7168]{1,0:T(8,128)(2,1)S(1)}, bf16[256,7168]{1,0:T(8,128)(2,1)}, u32[]{:S(2)}) copy-start(bf16[256,7168]{1,0:T(8,128)(2,1)} %copy-done.4) | copy-start | bytes 11010052
  59.8 30.2 %copy-start.8 = (s32[128,8]{0,1:T(8,128)S(1)}, s32[128,8]{0,1:T(8,128)}, u32[]{:S(2)}) copy-start(s32[128,8]{0,1:T(8,128)} %param.19) | copy-start | bytes 12292
  66.0 7.6 %collective-permute-start.23 = (bf16[32,7296]{1,0:T(8,128)(2,1)S(1)}, bf16[32,7296]{1,0:T(8,128)(2,1)S(1)}, u32[]{:S(2)}, u32[]{:S(2)}) collective-permute-start(bf16[32,7296]{1,0:T(8,128)(2,1)S(1)} %get-tuple-element.39), channel_id=1, source_target_pairs={{0,4},{4,0},{8,12},{12,8},{16,20},{20,16},{24,28},{28,24},{1,5},{5... | collective-permute-start | bytes 1400840 | tf_op jit(solution)/shard_map/ppermute | solution.py:21
  66.2 5.5 %collective-permute-start.10 = (bf16[64,512]{1,0:T(8,128)(2,1)S(1)}, bf16[64,512]{1,0:T(8,128)(2,1)S(1)}, u32[]{:S(2)}, u32[]{:S(2)}) collective-permute-start(bf16[64,512]{1,0:T(8,128)(2,1)S(1)} %get-tuple-element.53), channel_id=1, source_target_pairs={{0,24},{4,28},{8,16},{12,20},{16,8},{20,12},{24,0},{28,4},{1,25},{... | collective-permute-start | bytes 196616 | tf_op jit(solution)/shard_map/ppermute | solution.py:31
  67.8 5.2 %collective-permute-start.9 = (bf16[64,512]{1,0:T(8,128)(2,1)S(1)}, bf16[64,512]{1,0:T(8,128)(2,1)S(1)}, u32[]{:S(2)}, u32[]{:S(2)}) collective-permute-start(bf16[64,512]{1,0:T(8,128)(2,1)S(1)} %get-tuple-element.54), channel_id=1, source_target_pairs={{0,16},{4,12},{8,24},{12,4},{16,0},{20,28},{24,8},{28,20},{1,17},{... | collective-permute-start | bytes 196616 | tf_op jit(solution)/shard_map/ppermute | solution.py:31
  69.3 4.3 %collective-permute-start.8 = (bf16[64,512]{1,0:T(8,128)(2,1)S(1)}, bf16[64,512]{1,0:T(8,128)(2,1)S(1)}, u32[]{:S(2)}, u32[]{:S(2)}) collective-permute-start(bf16[64,512]{1,0:T(8,128)(2,1)S(1)} %get-tuple-element.52), channel_id=1, source_target_pairs={{0,8},{4,20},{8,0},{12,28},{16,24},{20,4},{24,16},{28,12},{1,9},{5... | collective-permute-start | bytes 196616 | tf_op jit(solution)/shard_map/ppermute | solution.py:31
  73.6 4.3 %collective-permute-start.11 = (bf16[64,512]{1,0:T(8,128)(2,1)S(1)}, bf16[64,512]{1,0:T(8,128)(2,1)S(1)}, u32[]{:S(2)}, u32[]{:S(2)}) collective-permute-start(bf16[64,512]{1,0:T(8,128)(2,1)S(1)} %add_convert_fusion.3), channel_id=1, source_target_pairs={{0,1},{1,0},{2,3},{3,2},{4,5},{5,4},{6,7},{7,6},{8,9},{9,8},{10,11... | collective-permute-start | bytes 196616 | tf_op jit(solution)/shard_map/ppermute | solution.py:21
  73.8 5.1 %collective-permute-start.24 = (bf16[8,7296]{1,0:T(8,128)(2,1)S(1)}, bf16[8,7296]{1,0:T(8,128)(2,1)S(1)}, u32[]{:S(2)}, u32[]{:S(2)}) collective-permute-start(bf16[8,7296]{1,0:T(8,128)(2,1)S(1)} %get-tuple-element.41), channel_id=1, source_target_pairs={{0,8},{4,20},{8,0},{12,28},{16,24},{20,4},{24,16},{28,12},{1,9},{5... | collective-permute-start | bytes 350216 | tf_op jit(solution)/shard_map/ppermute | solution.py:31
  74.8 5.1 %collective-permute-start.25 = (bf16[8,7296]{1,0:T(8,128)(2,1)S(1)}, bf16[8,7296]{1,0:T(8,128)(2,1)S(1)}, u32[]{:S(2)}, u32[]{:S(2)}) collective-permute-start(bf16[8,7296]{1,0:T(8,128)(2,1)S(1)} %get-tuple-element.42), channel_id=1, source_target_pairs={{0,16},{4,12},{8,24},{12,4},{16,0},{20,28},{24,8},{28,20},{1,17},{... | collective-permute-start | bytes 350216 | tf_op jit(solution)/shard_map/ppermute | solution.py:31
  75.4 6.8 %collective-permute-start.26 = (bf16[8,7296]{1,0:T(8,128)(2,1)S(1)}, bf16[8,7296]{1,0:T(8,128)(2,1)S(1)}, u32[]{:S(2)}, u32[]{:S(2)}) collective-permute-start(bf16[8,7296]{1,0:T(8,128)(2,1)S(1)} %get-tuple-element.43), channel_id=1, source_target_pairs={{0,24},{4,28},{8,16},{12,20},{16,8},{20,12},{24,0},{28,4},{1,25},{... | collective-permute-start | bytes 350216 | tf_op jit(solution)/shard_map/ppermute | solution.py:31
  77.9 8.8 %collective-permute-start.12 = (bf16[64,512]{1,0:T(8,128)(2,1)S(1)}, bf16[64,512]{1,0:T(8,128)(2,1)S(1)}, u32[]{:S(2)}, u32[]{:S(2)}) collective-permute-start(bf16[64,512]{1,0:T(8,128)(2,1)S(1)} %add_convert_fusion.2), channel_id=1, source_target_pairs={{0,2},{1,3},{2,0},{3,1},{4,6},{5,7},{6,4},{7,5},{8,10},{9,11},{10,... | collective-permute-start | bytes 196616 | tf_op jit(solution)/shard_map/ppermute | solution.py:21
  82.3 5.1 %collective-permute-start.27 = (bf16[2,7296]{1,0:T(2,128)(2,1)S(1)}, bf16[2,7296]{1,0:T(2,128)(2,1)S(1)}, u32[]{:S(2)}, u32[]{:S(2)}) collective-permute-start(bf16[2,7296]{1,0:T(2,128)(2,1)S(1)} %get-tuple-element.45), channel_id=1, source_target_pairs={{0,1},{1,0},{2,3},{3,2},{4,5},{5,4},{6,7},{7,6},{8,9},{9,8},{10,11... | collective-permute-start | bytes 87560 | tf_op jit(solution)/shard_map/ppermute | solution.py:21
  84.3 4.8 %collective-permute-start.28 = (bf16[2,7296]{1,0:T(2,128)(2,1)S(1)}, bf16[2,7296]{1,0:T(2,128)(2,1)S(1)}, u32[]{:S(2)}, u32[]{:S(2)}) collective-permute-start(bf16[2,7296]{1,0:T(2,128)(2,1)S(1)} %get-tuple-element.46), channel_id=1, source_target_pairs={{0,2},{1,3},{2,0},{3,1},{4,6},{5,7},{6,4},{7,5},{8,10},{9,11},{10,... | collective-permute-start | bytes 87560 | tf_op jit(solution)/shard_map/ppermute | solution.py:21
  84.3 5.7 %collective-permute-start.29 = (bf16[2,7296]{1,0:T(2,128)(2,1)S(1)}, bf16[2,7296]{1,0:T(2,128)(2,1)S(1)}, u32[]{:S(2)}, u32[]{:S(2)}) collective-permute-start(bf16[2,7296]{1,0:T(2,128)(2,1)S(1)} %get-tuple-element.47), channel_id=1, source_target_pairs={{0,3},{1,2},{2,1},{3,0},{4,7},{5,6},{6,5},{7,4},{8,11},{9,10},{10,... | collective-permute-start | bytes 87560 | tf_op jit(solution)/shard_map/ppermute | solution.py:21
where the time goes:
time: 92.5 us; the launch traced here: 92.2 us
  starting transfers between devices  30.5 us (33%)
  waiting for transfers between devices  28.2 us (30%)
  Pallas kernels  18 us (19%)
  local copies, waits for them, and re-layouts  12.2 us (13%)
  other arithmetic  2.43 us (3%)
    pallas_call x6, Pallas kernels, call(): pl.pallas_call(body, out_shape=outs, in_specs=in_specs, out_specs=out_spe...  18 us
    ppermute x12, waiting for transfers between devices, chip_exchange(): return lax.ppermute(array, 'ctx', pairs)  17.3 us
    ppermute x18, starting transfers between devices, exchange(): return lax.ppermute(array, axis, [(i, i ^ mask) for i in range(count)])  15.3 us
    ppermute x12, starting transfers between devices, chip_exchange(): return lax.ppermute(array, 'ctx', pairs)  15.2 us
    unnamed x18, local copies, waits for them, and re-layouts  11.6 us
    ppermute x18, waiting for transfers between devices, exchange(): return lax.ppermute(array, axis, [(i, i ^ mask) for i in range(count)])  11 us
  transfers between devices with their start and end apart: 30, of which 17 were waited for; matrix products, arithmetic and copies ran while one was open for 1% of the time, Pallas kernels for 11%

commit v1 on v0

--- a/solution.py
+++ b/solution.py
@@ -68,6 +68,10 @@
     )(*args)
 
 
+def halvings(count):
+    return [count >> i for i in range(1, count.bit_length())]
+
+
 def slot_experts(shape):
     slot = lax.broadcasted_iota(jnp.int32, shape, 0)
     return (slot >> (CAP.bit_length() - 1)) ^ lax.axis_index("exp")
@@ -76,7 +80,7 @@
 def route_body(n_exp, ids_hbm, order_hbm, gates_hbm, tok_hbm, grad_hbm, *rest):
     msgs = rest[:n_exp]
     weight_ref, chosen_ref, ids_ref, order_ref, gates_ref, held, sems = rest[n_exp:]
-    pieces = 2
+    pieces = 4
     width = held.shape[2]
     piece = width // pieces
     small = [
@@ -143,7 +147,7 @@
             pltpu.VMEM((1, rows), jnp.int32),
             pltpu.VMEM((top, rows), F32),
             pltpu.VMEM((2, rows, width), BF16),
-            pltpu.SemaphoreType.DMA((7,)),
+            pltpu.SemaphoreType.DMA((11,)),
         ],
         12 * MIB,
         flops=4 * n_exp * CAP * rows * width,
@@ -151,26 +155,28 @@
     return res[:n_exp], res[n_exp], res[n_exp + 1]
 
 
-def attention_body(n_ctx, heads, row_block, *refs):
+def attention_body(n_blocks, heads, row_block, *refs):
     q_ref, go_ref = refs[:2]
-    blocks = refs[2 : 2 + n_ctx]
-    w_hbm = refs[2 + n_ctx : 5 + n_ctx]
-    dq_hbm, even_ref, odd_ref = refs[5 + n_ctx : 8 + n_ctx]
-    w_vmem = refs[8 + n_ctx : 11 + n_ctx]
-    lat, dq, dq_sems, w_sems = refs[11 + n_ctx :]
+    blocks = refs[2 : 2 + n_blocks]
+    w_hbm = refs[2 + n_blocks : 5 + n_blocks]
+    dq_hbm, even_ref, odd_ref = refs[5 + n_blocks : 8 + n_blocks]
+    w_vmem = refs[8 + n_blocks : 11 + n_blocks]
+    lat, dq, dq_sems, w_sems = refs[11 + n_blocks :]
     fetches = [
         pltpu.make_async_copy(src.at[0], dst, w_sems.at[i])
         for i, (src, dst) in enumerate(zip(w_hbm, w_vmem))
     ]
     for fetch in fetches:
         fetch.start()
-    per = blocks[0].shape[0]
     rows, width = q_ref.shape
+    per = rows // heads
     scale = SCALE_DIM ** (-0.5)
     keydoc = []
-    for i, block in enumerate(blocks):
-        lat[i * per : (i + 1) * per, :] = block[:, :width]
+    at = 0
+    for block in blocks:
+        lat[at : at + block.shape[0], :] = block[:, :width]
         keydoc.append(block[:, width:].astype(F32))
+        at += block.shape[0]
     keydoc = jnp.concatenate(keydoc, axis=0)
     reps = row_block // LANES
     if reps > 1:
@@ -189,7 +195,7 @@
         at = col + b * row_block
         spread = jnp.where((at >= owner * heads) & (at < (owner + 1) * heads), 1.0, 0.0)
         qdoc = lax.dot_general(
-            blocks[0][:, width:], spread.astype(BF16), tn, preferred_element_type=F32
+            blocks[0][:per, width:], spread.astype(BF16), tn, preferred_element_type=F32
         )[:1]
         scores = lax.dot_general(keys, q, nt, preferred_element_type=F32) * scale
         scores = jnp.where(keydoc == qdoc, scores, -1e30)
@@ -218,11 +224,11 @@
 
 
 def attention(queries, grad_out, blocks, weights):
-    n_ctx = len(blocks)
+    n_blocks = len(blocks)
     q_rows, heads, width = queries.shape
     rows = q_rows * heads
-    keys = blocks[0].shape[0] * n_ctx
-    row_block = min(256, rows)
+    keys = sum(block.shape[0] for block in blocks)
+    row_block = min(1024, rows)
     q = queries.reshape(rows, width)
     go = grad_out.reshape(rows, width)
     half = (keys // 2, width)
@@ -233,10 +239,10 @@
     ]
     outs += [pltpu.VMEM(w.shape[1:], BF16) for w in weights]
     res = call(
-        functools.partial(attention_body, n_ctx, heads, row_block),
+        functools.partial(attention_body, n_blocks, heads, row_block),
         outs,
         (q, go, *blocks, *weights),
-        [vmem_spec()] * (2 + n_ctx) + [hbm_spec()] * 3,
+        [vmem_spec()] * (2 + n_blocks) + [hbm_spec()] * 3,
         [
             pltpu.VMEM((keys, width), BF16),
             pltpu.VMEM((rows, width), BF16),
@@ -259,7 +265,7 @@
 def expert_body(n_ctx, chunks, *refs):
     blocks = refs[:n_ctx]
     wg, wu, wd, even_ref, odd_ref, xt, xg = refs[n_ctx:]
-    width, hid = wg.shape
+    hid, width = wd.shape
     step = width // chunks
     per = blocks[0].shape[0] // 2
     for i, block in enumerate(blocks):
@@ -286,7 +292,7 @@
     tail = split_score(score, lane)
     even_ref[:, pl.ds(width, LANES)] = tail[:half]
     odd_ref[:, pl.ds(width, LANES)] = tail[half:]
-    fine = 512
+    fine = 1024
     for c in range(width // fine):
         cols = pl.ds(c * fine, fine)
         part = lax.dot_general(ggrad, wg[cols, :], nt, preferred_element_type=F32)
@@ -304,7 +310,7 @@
     out = jax.ShapeDtypeStruct((rows // 2, width + LANES), BF16)
     weights = [pltpu.with_memory_space_constraint(w, pltpu.VMEM) for w in weights]
     return call(
-        functools.partial(expert_body, n_ctx, 4),
+        functools.partial(expert_body, n_ctx, 7),
         [out, out],
         (*blocks, *weights),
         [vmem_spec()] * (n_ctx + 3),
@@ -370,7 +376,11 @@
 
 def final_body(n_exp, chunks, *refs):
     msgs = refs[:n_exp]
-    weight_ref, chosen_ref, ids_ref, dtok_hbm, dgate_ref, out, sems = refs[n_exp:]
+    weight_ref, chosen_ref, ids_ref, mine_ref, other_ref = refs[n_exp : n_exp + 5]
+    dtok_hbm, dgate_ref, dlat_hbm, out, dlat, sems = refs[n_exp + 5 :]
+    dlat[...] = (mine_ref[...].astype(F32) + other_ref[...].astype(F32)).astype(BF16)
+    dlat_write = pltpu.make_async_copy(dlat, dlat_hbm, sems.at[chunks])
+    dlat_write.start()
     width = msgs[0].shape[1] - LANES
     top, rows = ids_ref.shape
     slots = n_exp * CAP
@@ -382,7 +392,7 @@
     lhs = jnp.concatenate([high, mid, low], axis=0)
     tn = (((0,), (0,)), ((), ()))
     step = width // chunks
-    writes = []
+    writes = [dlat_write]
     for c in range(chunks):
         cols = pl.ds(c * step, step)
         piece = jnp.concatenate([msg[:, cols] for msg in msgs], axis=0)
@@ -404,25 +414,30 @@
         write.wait()
 
 
-def final(msgs, weight, chosen, expert_ids):
+def final(msgs, weight, chosen, expert_ids, lat_mine, lat_other):
     n_exp = len(msgs)
     width = msgs[0].shape[1] - LANES
     rows, top = expert_ids.shape
-    chunks = 4
-    d_tokens, d_gates = call(
+    chunks = 7
+    d_tokens, d_gates, d_latent = call(
         functools.partial(final_body, n_exp, chunks),
         [
             jax.ShapeDtypeStruct((rows, width), BF16),
             jax.ShapeDtypeStruct((top, rows), BF16),
+            jax.ShapeDtypeStruct(lat_mine.shape, BF16),
         ],
-        (*msgs, weight, chosen, expert_ids.T),
-        [vmem_spec()] * (n_exp + 3),
-        [pltpu.VMEM((rows, width), BF16), pltpu.SemaphoreType.DMA((chunks,))],
+        (*msgs, weight, chosen, expert_ids.T, lat_mine, lat_other),
+        [vmem_spec()] * (n_exp + 5),
+        [
+            pltpu.VMEM((rows, width), BF16),
+            pltpu.VMEM(lat_mine.shape, BF16),
+            pltpu.SemaphoreType.DMA((chunks + 1,)),
+        ],
         12 * MIB,
         flops=6 * n_exp * CAP * rows * width,
-        out_specs=[hbm_spec(), vmem_spec()],
-    )
-    return d_tokens, d_gates.T
+        out_specs=[hbm_spec(), vmem_spec(), hbm_spec()],
+    )
+    return d_tokens, d_gates.T, d_latent
 
 
 def gather_blocks(own, n_ctx):
@@ -471,15 +486,15 @@
     d_queries, lat_even, lat_odd, weights = attention(
         queries, grad_out, lat_blocks, (w_gate, w_up, w_down)
     )
-    lat_sum = widen_add(lat_even, core_exchange(lat_odd))
-    lat_parts = [lat_sum[:per_dev]]
-    for p in range(1, chips):
-        part = lat_sum[p * per_dev : (p + 1) * per_dev]
-        lat_parts.append(chip_exchange(part, p))
-    lat_total = widen_add(*lat_parts)
+    lat_total = widen_add(lat_even, core_exchange(lat_odd))
+    for p in halvings(chips):
+        keep, send = lat_total[: p * per_dev], lat_total[p * per_dev :]
+        lat_total = widen_add(keep, chip_exchange(send, p))
     mask = 1
     while mask < n_exp:
-        lat_total = widen_add(lat_total, exchange(lat_total, "exp", mask))
+        if mask > 1:
+            lat_total = widen_add(lat_total, lat_other)
+        lat_other = exchange(lat_total, "exp", mask)
         mask *= 2
 
     even, odd = experts(row_blocks, weights)
@@ -487,8 +502,10 @@
     parts = [summed[0]] + [chip_exchange(summed[p], p) for p in range(1, chips)]
     backs = owner_sum(parts, n_exp)
     back = [backs[0]] + [exchange(backs[k], "exp", k) for k in range(1, n_exp)]
-    d_tokens, d_gates = final(back, weight, chosen, expert_ids)
-    return (d_queries, lat_total, d_tokens, d_gates)
+    d_tokens, d_gates, d_latent = final(
+        back, weight, chosen, expert_ids, lat_total, lat_other
+    )
+    return (d_queries, d_latent, d_tokens, d_gates)
 
 
 def solution(mesh):

time: 92.5 us -> 89.5 us (0.968)
  Pallas kernels: 18 us -> 16 us
  starting transfers between devices: 30.5 us -> 29.1 us
  waiting for transfers between devices: 28.2 us -> 29.4 us
    ppermute x18, waiting for transfers between devices: 11 us -> 14.2 us  [exchange(): return lax.ppermute(array, axis, [(i, i ^ mask) for i in range(count)])]
    pallas_call x6, Pallas kernels: 18 us -> 16 us  [call(): pl.pallas_call(body, out_shape=outs, in_specs=in_specs, out_specs=out_spe...]
    ppermute x12 -> x11, waiting for transfers between devices: 17.3 us -> 15.3 us  [chip_exchange(): return lax.ppermute(array, 'ctx', pairs)]
    ppermute x12 -> x11, starting transfers between devices: 15.2 us -> 13.7 us  [chip_exchange(): return lax.ppermute(array, 'ctx', pairs)]
  transfers between devices with their start and end apart: 30 -> 29, of which waited for: 17 -> 13; matrix products, arithmetic and copies ran while one was open for 1% -> 1% of each run, Pallas kernels for 11% -> 16%
where the time goes in v1:
time: 89.5 us; the launch traced here: 89.3 us
  waiting for transfers between devices  29.4 us (33%)
  starting transfers between devices  29.1 us (33%)
  Pallas kernels  16 us (18%)
  local copies, waits for them, and re-layouts  12.2 us (14%)
  other arithmetic  1.8 us (2%)
    pallas_call x6, Pallas kernels, call(): pl.pallas_call(body, out_shape=outs, in_specs=in_specs, out_specs=out_spe...  16 us
    ppermute x18, starting transfers between devices, exchange(): return lax.ppermute(array, axis, [(i, i ^ mask) for i in range(count)])  15.4 us
    ppermute x11, waiting for transfers between devices, chip_exchange(): return lax.ppermute(array, 'ctx', pairs)  15.3 us
    ppermute x18, waiting for transfers between devices, exchange(): return lax.ppermute(array, axis, [(i, i ^ mask) for i in range(count)])  14.2 us
    ppermute x11, starting transfers between devices, chip_exchange(): return lax.ppermute(array, 'ctx', pairs)  13.7 us
    unnamed x18, local copies, waits for them, and re-layouts  11.6 us
  transfers between devices with their start and end apart: 29, of which 13 were waited for; matrix products, arithmetic and copies ran while one was open for 1% of the time, Pallas kernels for 16%

profile of v1, /device:TPU:0, one launch (start us, length us, event | category | flops | bytes accessed | tf_op | source)
XLA Modules:
  0.0 89.3 jit_solution(11775839194306246083)
XLA Ops:
  0.7 0.8 convert_element_type.39
  1.5 0.1 broadcast_in_dim.2
  1.5 0.9 pad_maximum_fusion.refs_2_
  2.4 3.0 %collective-permute-start = (bf16[64,640]{1,0:T(8,128)(2,1)S(1)}, bf16[64,640]{1,0:T(8,128)(2,1)S(1)}, u32[]{:S(2)}, u32[]{:S(2)}) collective-permute-start(bf16[64,640]{1,0:T(8,128)(2,1)S(1)} %pad_maximum_fusion.refs_2_), channel_id=1, source_target_pairs={{0,8},{4,20},{8,0},{12,28},{16,24},{20,4},{24,16},{28,12},{1,9},{5... | collective-permute-start | bytes 245768 | tf_op jit(solution)/shard_map/ppermute | solution.py:31
  5.4 1.5 %collective-permute-start.1 = (bf16[64,640]{1,0:T(8,128)(2,1)S(1)}, bf16[64,640]{1,0:T(8,128)(2,1)S(1)}, u32[]{:S(2)}, u32[]{:S(2)}) collective-permute-start(bf16[64,640]{1,0:T(8,128)(2,1)S(1)} %pad_maximum_fusion.refs_2_), channel_id=1, source_target_pairs={{0,16},{4,12},{8,24},{12,4},{16,0},{20,28},{24,8},{28,20},{1,17},{... | collective-permute-start | bytes 245768 | tf_op jit(solution)/shard_map/ppermute | solution.py:31
  6.9 0.0 collective-permute-start.2
  6.9 0.0 collective-permute-start.3
  6.9 2.4 %shard_map.148 = (bf16[4,7168]{1,0:T(4,128)(2,1)S(1)}, bf16[4,7168]{1,0:T(4,128)(2,1)S(1)}, bf16[4,7168]{1,0:T(4,128)(2,1)S(1)}, bf16[4,7168]{1,0:T(4,128)(2,1)S...) custom-call(s32[8,128]{1,0:T(8,128)} %bitcast.8, s32[1,128]{1,0:T(1,128)} %order_hbm.1, f32[8,128]{1,0:T(8,128)} %bitcast.10, ...), custom_call_target="tpu_custom_call" | custom-call | flops 29360128 | bytes 3916288 | tf_op jit(solution)/shard_map/pallas_call | solution.py:60
  9.3 4.1 %collective-permute-start.9 = (bf16[4,7168]{1,0:T(4,128)(2,1)S(1)}, bf16[4,7168]{1,0:T(4,128)(2,1)S(1)}, u32[]{:S(2)}, u32[]{:S(2)}) collective-permute-start(bf16[4,7168]{1,0:T(4,128)(2,1)S(1)} %get-tuple-element.33), channel_id=1, source_target_pairs={{0,3},{1,2},{2,1},{3,0},{4,7},{5,6},{6,5},{7,4},{8,11},{9,10},{10,... | collective-permute-start | bytes 172040 | tf_op jit(solution)/shard_map/ppermute | solution.py:21
  13.4 2.6 %collective-permute-done.9 = bf16[4,7168]{1,0:T(4,128)(2,1)S(1)} collective-permute-done((bf16[4,7168]{1,0:T(4,128)(2,1)S(1)}, bf16[4,7168]{1,0:T(4,128)(2,1)S(1)}, u32[]{:S(2)}, u32[]{:S(2)}) %collective-permute-start.9) | collective-permute-done | bytes 57376 | tf_op jit(solution)/shard_map/ppermute | solution.py:21
  16.1 0.6 collective-permute-start.8
  16.8 5.2 %collective-permute-done.8 = bf16[4,7168]{1,0:T(4,128)(2,1)S(1)} collective-permute-done((bf16[4,7168]{1,0:T(4,128)(2,1)S(1)}, bf16[4,7168]{1,0:T(4,128)(2,1)S(1)}, u32[]{:S(2)}, u32[]{:S(2)}) %collective-permute-start.8) | collective-permute-done | bytes 57376 | tf_op jit(solution)/shard_map/ppermute | solution.py:21
  21.9 0.3 collective-permute-start.7
  22.3 0.0 collective-permute-done.refs_3_
  22.3 0.0 collective-permute-start.4
  22.3 0.5 collective-permute-start.5
  22.8 0.0 collective-permute-done.2.refs_5_
  22.8 0.1 collective-permute-start.6
  22.9 0.6 collective-permute-done.4.refs_7_
  23.5 0.2 collective-permute-done.5.refs_8_
  23.7 0.4 collective-permute-done.6.refs_9_
  24.1 5.2 %shard_map.147 = (bf16[1024,512]{1,0:T(8,128)(2,1)}, bf16[256,512]{1,0:T(8,128)(2,1)S(1)}, bf16[256,512]{1,0:T(8,128)(2,1)S(1)}, bf16[7168,256]{1,0:T(8,128)(2,1...) custom-call(bf16[1024,512]{1,0:T(8,128)(2,1)S(1)} %bitcast.6, bf16[1024,512]{1,0:T(8,128)(2,1)S(1)} %bitcast.7, ...), custom_call_target="tpu_custom_call" | custom-call | flops 2684354560 | bytes 26345472 | tf_op jit(solution)/shard_map/pallas_call | solution.py:60
  29.3 1.8 %copy-done = bf16[7168,256]{1,0:T(8,128)(2,1)} copy-done((bf16[7168,256]{1,0:T(8,128)(2,1)}, bf16[7168,256]{1,0:T(8,128)(2,1)S(1)}, u32[]{:S(2)}) %copy-start) | copy-done | bytes 3670040
  31.1 1.8 %copy-done.2 = bf16[7168,256]{1,0:T(8,128)(2,1)} copy-done((bf16[7168,256]{1,0:T(8,128)(2,1)}, bf16[7168,256]{1,0:T(8,128)(2,1)S(1)}, u32[]{:S(2)}) %copy-start.2) | copy-done | bytes 3670040
  32.9 1.9 %copy-done.4 = bf16[256,7168]{1,0:T(8,128)(2,1)} copy-done((bf16[256,7168]{1,0:T(8,128)(2,1)}, bf16[256,7168]{1,0:T(8,128)(2,1)S(1)}, u32[]{:S(2)}) %copy-start.4) | copy-done | bytes 3670040
  34.8 0.2 collective-permute-start.24
  35.0 0.3 concatenate.7.refs_0_
  35.3 1.6 %collective-permute-start.10 = (bf16[16,7168]{1,0:T(8,128)(2,1)S(1)}, bf16[16,7168]{1,0:T(8,128)(2,1)S(1)}, u32[]{:S(2)}, u32[]{:S(2)}) collective-permute-start(bf16[16,7168]{1,0:T(8,128)(2,1)S(1)} %concatenate.7.refs_0_), channel_id=1, source_target_pairs={{0,8},{4,20},{8,0},{12,28},{16,24},{20,4},{24,16},{28,12},{1,9},{5... | collective-permute-start | bytes 688136 | tf_op jit(solution)/shard_map/ppermute | solution.py:31
  36.9 1.5 %collective-permute-start.11 = (bf16[16,7168]{1,0:T(8,128)(2,1)S(1)}, bf16[16,7168]{1,0:T(8,128)(2,1)S(1)}, u32[]{:S(2)}, u32[]{:S(2)}) collective-permute-start(bf16[16,7168]{1,0:T(8,128)(2,1)S(1)} %concatenate.7.refs_0_), channel_id=1, source_target_pairs={{0,16},{4,12},{8,24},{12,4},{16,0},{20,28},{24,8},{28,20},{1,17},{... | collective-permute-start | bytes 688136 | tf_op jit(solution)/shard_map/ppermute | solution.py:31
  38.4 0.5 collective-permute-start.12
  38.9 0.0 collective-permute-start.13
  38.9 4.4 %collective-permute-done.10.refs_1_ = bf16[16,7168]{1,0:T(8,128)(2,1)S(1)} collective-permute-done((bf16[16,7168]{1,0:T(8,128)(2,1)S(1)}, bf16[16,7168]{1,0:T(8,128)(2,1)S(1)}, u32[]{:S(2)}, u32[]{:S(2)}) %collective-permute-start.10) | collective-permute-done | bytes 229408 | tf_op jit(solution)/shard_map/ppermute | solution.py:31
  43.2 0.0 collective-permute-start.14
  43.2 0.0 collective-permute-done.11.refs_2_
  43.2 1.1 %collective-permute-start.15 = (bf16[16,7168]{1,0:T(8,128)(2,1)S(1)}, bf16[16,7168]{1,0:T(8,128)(2,1)S(1)}, u32[]{:S(2)}, u32[]{:S(2)}) collective-permute-start(bf16[16,7168]{1,0:T(8,128)(2,1)S(1)} %collective-permute-done.11.refs_2_), channel_id=1, source_target_pairs={{0,4},{4,0},{8,12},{12,8},{16,20},{20,16},{24,28},{28,24},{1,5},{5... | collective-permute-start | bytes 688136 | tf_op jit(solution)/shard_map/ppermute | solution.py:21
  44.3 5.0 %collective-permute-done.12.refs_3_ = bf16[16,7168]{1,0:T(8,128)(2,1)S(1)} collective-permute-done((bf16[16,7168]{1,0:T(8,128)(2,1)S(1)}, bf16[16,7168]{1,0:T(8,128)(2,1)S(1)}, u32[]{:S(2)}, u32[]{:S(2)}) %collective-permute-start.12) | collective-permute-done | bytes 229408 | tf_op jit(solution)/shard_map/ppermute | solution.py:31
  49.3 0.0 collective-permute-start.16
  49.3 0.0 collective-permute-done.24
  49.4 0.1 add_convert_fusion
  49.4 0.8 collective-permute-start.25
  50.2 0.0 collective-permute-done.13.refs_4_
  50.2 0.6 collective-permute-done.16.refs_7_
  50.8 2.0 %copy-done.1 = bf16[7168,256]{1,0:T(8,128)(2,1)S(1)} copy-done((bf16[7168,256]{1,0:T(8,128)(2,1)S(1)}, bf16[7168,256]{1,0:T(8,128)(2,1)}, u32[]{:S(2)}) %copy-start.1) | copy-done | bytes 3670040
  52.9 2.0 %copy-done.3 = bf16[7168,256]{1,0:T(8,128)(2,1)S(1)} copy-done((bf16[7168,256]{1,0:T(8,128)(2,1)S(1)}, bf16[7168,256]{1,0:T(8,128)(2,1)}, u32[]{:S(2)}) %copy-start.3) | copy-done | bytes 3670040
  54.9 2.0 %copy-done.5 = bf16[256,7168]{1,0:T(8,128)(2,1)S(1)} copy-done((bf16[256,7168]{1,0:T(8,128)(2,1)S(1)}, bf16[256,7168]{1,0:T(8,128)(2,1)}, u32[]{:S(2)}) %copy-start.5) | copy-done | bytes 3670040
  57.0 6.0 %shard_map.149 = (bf16[32,7296]{1,0:T(8,128)(2,1)S(1)}, bf16[32,7296]{1,0:T(8,128)(2,1)S(1)}) custom-call(bf16[16,7168]{1,0:T(8,128)(2,1)S(1)} %concatenate.7.refs_0_, bf16[16,7168]{1,0:T(8,128)(2,1)S(1)} %collective-permute-done.10.refs_1_, bf16[16,7168]{1,0:T(8,128)(2,1)S(1)} %collective-permute-done.11.refs_2_, ...), custom_call_target="tpu_custom_call" | custom-call | flops 1174405120 | bytes 13778944 | tf_op jit(solution)/shard_map/pallas_call | solution.py:60
  62.9 0.5 collective-permute-start.17
  63.5 1.3 %collective-permute-start.26 = (bf16[64,512]{1,0:T(8,128)(2,1)S(1)}, bf16[64,512]{1,0:T(8,128)(2,1)S(1)}, u32[]{:S(2)}, u32[]{:S(2)}) collective-permute-start(bf16[64,512]{1,0:T(8,128)(2,1)S(1)} %slice.57), channel_id=1, source_target_pairs={{0,8},{4,20},{8,0},{12,28},{16,24},{20,4},{24,16},{28,12},{1,9},{5... | collective-permute-start | bytes 196616 | tf_op jit(solution)/shard_map/ppermute | solution.py:31
  64.7 3.1 %collective-permute-done.26 = bf16[64,512]{1,0:T(8,128)(2,1)S(1)} collective-permute-done((bf16[64,512]{1,0:T(8,128)(2,1)S(1)}, bf16[64,512]{1,0:T(8,128)(2,1)S(1)}, u32[]{:S(2)}, u32[]{:S(2)}) %collective-permute-start.26) | collective-permute-done | bytes 65568 | tf_op jit(solution)/shard_map/ppermute | solution.py:31
  67.8 1.7 %collective-permute-start.27 = (bf16[64,512]{1,0:T(8,128)(2,1)S(1)}, bf16[64,512]{1,0:T(8,128)(2,1)S(1)}, u32[]{:S(2)}, u32[]{:S(2)}) collective-permute-start(bf16[64,512]{1,0:T(8,128)(2,1)S(1)} %add_convert_fusion.3), channel_id=1, source_target_pairs={{0,1},{1,0},{2,3},{3,2},{4,5},{5,4},{6,7},{7,6},{8,9},{9,8},{10,11... | collective-permute-start | bytes 196616 | tf_op jit(solution)/shard_map/ppermute | solution.py:21
  69.5 0.2 shard_map.150
  69.7 1.3 %collective-permute-start.18 = (bf16[8,7296]{1,0:T(8,128)(2,1)S(1)}, bf16[8,7296]{1,0:T(8,128)(2,1)S(1)}, u32[]{:S(2)}, u32[]{:S(2)}) collective-permute-start(bf16[8,7296]{1,0:T(8,128)(2,1)S(1)} %get-tuple-element.40), channel_id=1, source_target_pairs={{0,8},{4,20},{8,0},{12,28},{16,24},{20,4},{24,16},{28,12},{1,9},{5... | collective-permute-start | bytes 350216 | tf_op jit(solution)/shard_map/ppermute | solution.py:31
  71.0 0.6 collective-permute-start.19
  71.6 1.7 %collective-permute-start.20 = (bf16[8,7296]{1,0:T(8,128)(2,1)S(1)}, bf16[8,7296]{1,0:T(8,128)(2,1)S(1)}, u32[]{:S(2)}, u32[]{:S(2)}) collective-permute-start(bf16[8,7296]{1,0:T(8,128)(2,1)S(1)} %get-tuple-element.42), channel_id=1, source_target_pairs={{0,24},{4,28},{8,16},{12,20},{16,8},{20,12},{24,0},{28,4},{1,25},{... | collective-permute-start | bytes 350216 | tf_op jit(solution)/shard_map/ppermute | solution.py:31
  73.3 1.9 %collective-permute-start.28 = (bf16[64,512]{1,0:T(8,128)(2,1)S(1)}, bf16[64,512]{1,0:T(8,128)(2,1)S(1)}, u32[]{:S(2)}, u32[]{:S(2)}) collective-permute-start(bf16[64,512]{1,0:T(8,128)(2,1)S(1)} %add_convert_fusion.2.refs_7_), channel_id=1, source_target_pairs={{0,2},{1,3},{2,0},{3,1},{4,6},{5,7},{6,4},{7,5},{8,10},{9,11},{10,... | collective-permute-start | bytes 196616 | tf_op jit(solution)/shard_map/ppermute | solution.py:21
  75.2 0.3 collective-permute-done.18.refs_1_
  75.4 2.5 %collective-permute-done.19.refs_2_ = bf16[8,7296]{1,0:T(8,128)(2,1)S(1)} collective-permute-done((bf16[8,7296]{1,0:T(8,128)(2,1)S(1)}, bf16[8,7296]{1,0:T(8,128)(2,1)S(1)}, u32[]{:S(2)}, u32[]{:S(2)}) %collective-permute-start.19) | collective-permute-done | bytes 116768 | tf_op jit(solution)/shard_map/ppermute | solution.py:31
  78.0 0.1 shard_map.151
  78.1 0.4 collective-permute-start.21
  78.5 2.9 %collective-permute-start.22 = (bf16[2,7296]{1,0:T(2,128)(2,1)S(1)}, bf16[2,7296]{1,0:T(2,128)(2,1)S(1)}, u32[]{:S(2)}, u32[]{:S(2)}) collective-permute-start(bf16[2,7296]{1,0:T(2,128)(2,1)S(1)} %get-tuple-element.45), channel_id=1, source_target_pairs={{0,2},{1,3},{2,0},{3,1},{4,6},{5,7},{6,4},{7,5},{8,10},{9,11},{10,... | collective-permute-start | bytes 87560 | tf_op jit(solution)/shard_map/ppermute | solution.py:21
  81.4 1.1 %collective-permute-start.23 = (bf16[2,7296]{1,0:T(2,128)(2,1)S(1)}, bf16[2,7296]{1,0:T(2,128)(2,1)S(1)}, u32[]{:S(2)}, u32[]{:S(2)}) collective-permute-start(bf16[2,7296]{1,0:T(2,128)(2,1)S(1)} %get-tuple-element.46), channel_id=1, source_target_pairs={{0,3},{1,2},{2,1},{3,0},{4,7},{5,6},{6,5},{7,4},{8,11},{9,10},{10,... | collective-permute-start | bytes 87560 | tf_op jit(solution)/shard_map/ppermute | solution.py:21
  82.5 0.8 collective-permute-done.22.refs_2_
  83.3 3.8 %collective-permute-done.23.refs_3_ = bf16[2,7296]{1,0:T(2,128)(2,1)S(1)} collective-permute-done((bf16[2,7296]{1,0:T(2,128)(2,1)S(1)}, bf16[2,7296]{1,0:T(2,128)(2,1)S(1)}, u32[]{:S(2)}, u32[]{:S(2)}) %collective-permute-start.23) | collective-permute-done | bytes 29216 | tf_op jit(solution)/shard_map/ppermute | solution.py:21
  87.1 2.1 %shard_map.152 = (bf16[128,7168]{1,0:T(8,128)(2,1)}, bf16[8,128]{1,0:T(8,128)(2,1)}, bf16[64,512]{1,0:T(8,128)(2,1)}) custom-call(bf16[2,7296]{1,0:T(2,128)(2,1)S(1)} %get-tuple-element.43.refs_0_, bf16[2,7296]{1,0:T(2,128)(2,1)S(1)} %collective-permute-done.21.refs_1_, bf16[2,7296]{1,0:T(2,128)(2,1)S(1)} %collective-permute-done.22.refs_2_, ...), custom_call_target="tpu_custom_call" | custom-call | flops 44040192 | bytes 2162688 | tf_op jit(solution)/shard_map/pallas_call | solution.py:60
  (32 shorter events, 0.3 us)
Async XLA Ops:
  0.6 23.4 %copy-start.6 = (bf16[64,16,512]{2,1,0:T(8,128)(2,1)S(1)}, bf16[64,16,512]{2,1,0:T(8,128)(2,1)}, u32[]{:S(2)}) copy-start(bf16[64,16,512]{2,1,0:T(8,128)(2,1)} %param.12) | copy-start | bytes 3145732
  0.6 23.4 %copy-start.7 = (bf16[64,16,512]{2,1,0:T(8,128)(2,1)S(1)}, bf16[64,16,512]{2,1,0:T(8,128)(2,1)}, u32[]{:S(2)}) copy-start(bf16[64,16,512]{2,1,0:T(8,128)(2,1)} %param.14) | copy-start | bytes 3145732
  2.4 19.9 %collective-permute-start = (bf16[64,640]{1,0:T(8,128)(2,1)S(1)}, bf16[64,640]{1,0:T(8,128)(2,1)S(1)}, u32[]{:S(2)}, u32[]{:S(2)}) collective-permute-start(bf16[64,640]{1,0:T(8,128)(2,1)S(1)} %pad_maximum_fusion.refs_2_), channel_id=1, source_target_pairs={{0,8},{4,20},{8,0},{12,28},{16,24},{20,4},{24,16},{28,12},{1,9},{5... | collective-permute-start | bytes 245768 | tf_op jit(solution)/shard_map/ppermute | solution.py:31
  5.4 16.9 %collective-permute-start.1 = (bf16[64,640]{1,0:T(8,128)(2,1)S(1)}, bf16[64,640]{1,0:T(8,128)(2,1)S(1)}, u32[]{:S(2)}, u32[]{:S(2)}) collective-permute-start(bf16[64,640]{1,0:T(8,128)(2,1)S(1)} %pad_maximum_fusion.refs_2_), channel_id=1, source_target_pairs={{0,16},{4,12},{8,24},{12,4},{16,0},{20,28},{24,8},{28,20},{1,17},{... | collective-permute-start | bytes 245768 | tf_op jit(solution)/shard_map/ppermute | solution.py:31
  6.9 15.9 %collective-permute-start.2 = (bf16[64,640]{1,0:T(8,128)(2,1)S(1)}, bf16[64,640]{1,0:T(8,128)(2,1)S(1)}, u32[]{:S(2)}, u32[]{:S(2)}) collective-permute-start(bf16[64,640]{1,0:T(8,128)(2,1)S(1)} %pad_maximum_fusion.refs_2_), channel_id=1, source_target_pairs={{0,24},{4,28},{8,16},{12,20},{16,8},{20,12},{24,0},{28,4},{1,25},{... | collective-permute-start | bytes 245768 | tf_op jit(solution)/shard_map/ppermute | solution.py:31
  6.9 16.0 %collective-permute-start.3 = (bf16[64,640]{1,0:T(8,128)(2,1)S(1)}, bf16[64,640]{1,0:T(8,128)(2,1)S(1)}, u32[]{:S(2)}, u32[]{:S(2)}) collective-permute-start(bf16[64,640]{1,0:T(8,128)(2,1)S(1)} %pad_maximum_fusion.refs_2_), channel_id=1, source_target_pairs={{0,4},{4,0},{8,12},{12,8},{16,20},{20,16},{24,28},{28,24},{1,5},{5... | collective-permute-start | bytes 245768 | tf_op jit(solution)/shard_map/ppermute | solution.py:21
  9.3 6.8 %collective-permute-start.9 = (bf16[4,7168]{1,0:T(4,128)(2,1)S(1)}, bf16[4,7168]{1,0:T(4,128)(2,1)S(1)}, u32[]{:S(2)}, u32[]{:S(2)}) collective-permute-start(bf16[4,7168]{1,0:T(4,128)(2,1)S(1)} %get-tuple-element.33), channel_id=1, source_target_pairs={{0,3},{1,2},{2,1},{3,0},{4,7},{5,6},{6,5},{7,4},{8,11},{9,10},{10,... | collective-permute-start | bytes 172040 | tf_op jit(solution)/shard_map/ppermute | solution.py:21
  16.1 5.8 %collective-permute-start.8 = (bf16[4,7168]{1,0:T(4,128)(2,1)S(1)}, bf16[4,7168]{1,0:T(4,128)(2,1)S(1)}, u32[]{:S(2)}, u32[]{:S(2)}) collective-permute-start(bf16[4,7168]{1,0:T(4,128)(2,1)S(1)} %get-tuple-element.32), channel_id=1, source_target_pairs={{0,2},{1,3},{2,0},{3,1},{4,6},{5,7},{6,4},{7,5},{8,10},{9,11},{10,... | collective-permute-start | bytes 172040 | tf_op jit(solution)/shard_map/ppermute | solution.py:21
  21.9 13.0 %collective-permute-start.7 = (bf16[4,7168]{1,0:T(4,128)(2,1)S(1)}, bf16[4,7168]{1,0:T(4,128)(2,1)S(1)}, u32[]{:S(2)}, u32[]{:S(2)}) collective-permute-start(bf16[4,7168]{1,0:T(4,128)(2,1)S(1)} %get-tuple-element.31), channel_id=1, source_target_pairs={{0,1},{1,0},{2,3},{3,2},{4,5},{5,4},{6,7},{7,6},{8,9},{9,8},{10,11... | collective-permute-start | bytes 172040 | tf_op jit(solution)/shard_map/ppermute | solution.py:21
  22.3 1.3 %collective-permute-start.4 = (bf16[64,640]{1,0:T(8,128)(2,1)S(1)}, bf16[64,640]{1,0:T(8,128)(2,1)S(1)}, u32[]{:S(2)}, u32[]{:S(2)}) collective-permute-start(bf16[64,640]{1,0:T(8,128)(2,1)S(1)} %collective-permute-done.refs_3_), channel_id=1, source_target_pairs={{0,4},{4,0},{8,12},{12,8},{16,20},{20,16},{24,28},{28,24},{1,5},{5... | collective-permute-start | bytes 245768 | tf_op jit(solution)/shard_map/ppermute | solution.py:21
  22.3 1.4 %collective-permute-start.5 = (bf16[64,640]{1,0:T(8,128)(2,1)S(1)}, bf16[64,640]{1,0:T(8,128)(2,1)S(1)}, u32[]{:S(2)}, u32[]{:S(2)}) collective-permute-start(bf16[64,640]{1,0:T(8,128)(2,1)S(1)} %collective-permute-done.1.refs_4_), channel_id=1, source_target_pairs={{0,4},{4,0},{8,12},{12,8},{16,20},{20,16},{24,28},{28,24},{1,5},{5... | collective-permute-start | bytes 245768 | tf_op jit(solution)/shard_map/ppermute | solution.py:21
  22.8 1.3 %collective-permute-start.6 = (bf16[64,640]{1,0:T(8,128)(2,1)S(1)}, bf16[64,640]{1,0:T(8,128)(2,1)S(1)}, u32[]{:S(2)}, u32[]{:S(2)}) collective-permute-start(bf16[64,640]{1,0:T(8,128)(2,1)S(1)} %collective-permute-done.2.refs_5_), channel_id=1, source_target_pairs={{0,4},{4,0},{8,12},{12,8},{16,20},{20,16},{24,28},{28,24},{1,5},{5... | collective-permute-start | bytes 245768 | tf_op jit(solution)/shard_map/ppermute | solution.py:21
  29.3 1.8 %copy-start = (bf16[7168,256]{1,0:T(8,128)(2,1)}, bf16[7168,256]{1,0:T(8,128)(2,1)S(1)}, u32[]{:S(2)}) copy-start(bf16[7168,256]{1,0:T(8,128)(2,1)S(1)} %get-tuple-element.34.refs_8_) | copy-start | bytes 11010052
  31.1 1.8 %copy-start.2 = (bf16[7168,256]{1,0:T(8,128)(2,1)}, bf16[7168,256]{1,0:T(8,128)(2,1)S(1)}, u32[]{:S(2)}) copy-start(bf16[7168,256]{1,0:T(8,128)(2,1)S(1)} %get-tuple-element.35.refs_9_) | copy-start | bytes 11010052
  32.9 1.9 %copy-start.4 = (bf16[256,7168]{1,0:T(8,128)(2,1)}, bf16[256,7168]{1,0:T(8,128)(2,1)S(1)}, u32[]{:S(2)}) copy-start(bf16[256,7168]{1,0:T(8,128)(2,1)S(1)} %get-tuple-element.36.refs_10_) | copy-start | bytes 11010052
  34.8 14.6 %collective-permute-start.24 = (bf16[256,512]{1,0:T(8,128)(2,1)S(1)}, bf16[256,512]{1,0:T(8,128)(2,1)S(1)}, u32[]{:S(2)}, u32[]{:S(2)}) collective-permute-start(bf16[256,512]{1,0:T(8,128)(2,1)S(1)} %get-tuple-element.50), channel_id=1, source_target_pairs={{0,4},{4,0},{8,12},{12,8},{16,20},{20,16},{24,28},{28,24},{1,5},{5... | collective-permute-start | bytes 786440 | tf_op jit(solution)/shard_map/ppermute | solution.py:21
  35.3 7.9 %collective-permute-start.10 = (bf16[16,7168]{1,0:T(8,128)(2,1)S(1)}, bf16[16,7168]{1,0:T(8,128)(2,1)S(1)}, u32[]{:S(2)}, u32[]{:S(2)}) collective-permute-start(bf16[16,7168]{1,0:T(8,128)(2,1)S(1)} %concatenate.7.refs_0_), channel_id=1, source_target_pairs={{0,8},{4,20},{8,0},{12,28},{16,24},{20,4},{24,16},{28,12},{1,9},{5... | collective-permute-start | bytes 688136 | tf_op jit(solution)/shard_map/ppermute | solution.py:31
  36.9 6.4 %collective-permute-start.11 = (bf16[16,7168]{1,0:T(8,128)(2,1)S(1)}, bf16[16,7168]{1,0:T(8,128)(2,1)S(1)}, u32[]{:S(2)}, u32[]{:S(2)}) collective-permute-start(bf16[16,7168]{1,0:T(8,128)(2,1)S(1)} %concatenate.7.refs_0_), channel_id=1, source_target_pairs={{0,16},{4,12},{8,24},{12,4},{16,0},{20,28},{24,8},{28,20},{1,17},{... | collective-permute-start | bytes 688136 | tf_op jit(solution)/shard_map/ppermute | solution.py:31
  38.4 10.9 %collective-permute-start.12 = (bf16[16,7168]{1,0:T(8,128)(2,1)S(1)}, bf16[16,7168]{1,0:T(8,128)(2,1)S(1)}, u32[]{:S(2)}, u32[]{:S(2)}) collective-permute-start(bf16[16,7168]{1,0:T(8,128)(2,1)S(1)} %concatenate.7.refs_0_), channel_id=1, source_target_pairs={{0,24},{4,28},{8,16},{12,20},{16,8},{20,12},{24,0},{28,4},{1,25},{... | collective-permute-start | bytes 688136 | tf_op jit(solution)/shard_map/ppermute | solution.py:31
  38.9 11.3 %collective-permute-start.13 = (bf16[16,7168]{1,0:T(8,128)(2,1)S(1)}, bf16[16,7168]{1,0:T(8,128)(2,1)S(1)}, u32[]{:S(2)}, u32[]{:S(2)}) collective-permute-start(bf16[16,7168]{1,0:T(8,128)(2,1)S(1)} %concatenate.7.refs_0_), channel_id=1, source_target_pairs={{0,4},{4,0},{8,12},{12,8},{16,20},{20,16},{24,28},{28,24},{1,5},{5... | collective-permute-start | bytes 688136 | tf_op jit(solution)/shard_map/ppermute | solution.py:21
  43.2 7.0 %collective-permute-start.14 = (bf16[16,7168]{1,0:T(8,128)(2,1)S(1)}, bf16[16,7168]{1,0:T(8,128)(2,1)S(1)}, u32[]{:S(2)}, u32[]{:S(2)}) collective-permute-start(bf16[16,7168]{1,0:T(8,128)(2,1)S(1)} %collective-permute-done.10.refs_1_), channel_id=1, source_target_pairs={{0,4},{4,0},{8,12},{12,8},{16,20},{20,16},{24,28},{28,24},{1,5},{5... | collective-permute-start | bytes 688136 | tf_op jit(solution)/shard_map/ppermute | solution.py:21
  43.2 7.0 %collective-permute-start.15 = (bf16[16,7168]{1,0:T(8,128)(2,1)S(1)}, bf16[16,7168]{1,0:T(8,128)(2,1)S(1)}, u32[]{:S(2)}, u32[]{:S(2)}) collective-permute-start(bf16[16,7168]{1,0:T(8,128)(2,1)S(1)} %collective-permute-done.11.refs_2_), channel_id=1, source_target_pairs={{0,4},{4,0},{8,12},{12,8},{16,20},{20,16},{24,28},{28,24},{1,5},{5... | collective-permute-start | bytes 688136 | tf_op jit(solution)/shard_map/ppermute | solution.py:21
  49.3 1.5 %collective-permute-start.16 = (bf16[16,7168]{1,0:T(8,128)(2,1)S(1)}, bf16[16,7168]{1,0:T(8,128)(2,1)S(1)}, u32[]{:S(2)}, u32[]{:S(2)}) collective-permute-start(bf16[16,7168]{1,0:T(8,128)(2,1)S(1)} %collective-permute-done.12.refs_3_), channel_id=1, source_target_pairs={{0,4},{4,0},{8,12},{12,8},{16,20},{20,16},{24,28},{28,24},{1,5},{5... | collective-permute-start | bytes 688136 | tf_op jit(solution)/shard_map/ppermute | solution.py:21
  49.4 14.0 %collective-permute-start.25 = (bf16[128,512]{1,0:T(8,128)(2,1)S(1)}, bf16[128,512]{1,0:T(8,128)(2,1)S(1)}, u32[]{:S(2)}, u32[]{:S(2)}) collective-permute-start(bf16[128,512]{1,0:T(8,128)(2,1)S(1)} %slice.55), channel_id=1, source_target_pairs={{0,16},{4,12},{8,24},{12,4},{16,0},{20,28},{24,8},{28,20},{1,17},{... | collective-permute-start | bytes 393224 | tf_op jit(solution)/shard_map/ppermute | solution.py:31
  50.8 2.0 %copy-start.1 = (bf16[7168,256]{1,0:T(8,128)(2,1)S(1)}, bf16[7168,256]{1,0:T(8,128)(2,1)}, u32[]{:S(2)}) copy-start(bf16[7168,256]{1,0:T(8,128)(2,1)} %copy-done) | copy-start | bytes 11010052
  52.9 2.0 %copy-start.3 = (bf16[7168,256]{1,0:T(8,128)(2,1)S(1)}, bf16[7168,256]{1,0:T(8,128)(2,1)}, u32[]{:S(2)}) copy-start(bf16[7168,256]{1,0:T(8,128)(2,1)} %copy-done.2) | copy-start | bytes 11010052
  54.9 2.0 %copy-start.5 = (bf16[256,7168]{1,0:T(8,128)(2,1)S(1)}, bf16[256,7168]{1,0:T(8,128)(2,1)}, u32[]{:S(2)}) copy-start(bf16[256,7168]{1,0:T(8,128)(2,1)} %copy-done.4) | copy-start | bytes 11010052
  57.0 30.2 %copy-start.8 = (s32[128,8]{0,1:T(8,128)S(1)}, s32[128,8]{0,1:T(8,128)}, u32[]{:S(2)}) copy-start(s32[128,8]{0,1:T(8,128)} %param.19) | copy-start | bytes 12292
  62.9 6.6 %collective-permute-start.17 = (bf16[32,7296]{1,0:T(8,128)(2,1)S(1)}, bf16[32,7296]{1,0:T(8,128)(2,1)S(1)}, u32[]{:S(2)}, u32[]{:S(2)}) collective-permute-start(bf16[32,7296]{1,0:T(8,128)(2,1)S(1)} %get-tuple-element.38), channel_id=1, source_target_pairs={{0,4},{4,0},{8,12},{12,8},{16,20},{20,16},{24,28},{28,24},{1,5},{5... | collective-permute-start | bytes 1400840 | tf_op jit(solution)/shard_map/ppermute | solution.py:21
  63.5 4.3 %collective-permute-start.26 = (bf16[64,512]{1,0:T(8,128)(2,1)S(1)}, bf16[64,512]{1,0:T(8,128)(2,1)S(1)}, u32[]{:S(2)}, u32[]{:S(2)}) collective-permute-start(bf16[64,512]{1,0:T(8,128)(2,1)S(1)} %slice.57), channel_id=1, source_target_pairs={{0,8},{4,20},{8,0},{12,28},{16,24},{20,4},{24,16},{28,12},{1,9},{5... | collective-permute-start | bytes 196616 | tf_op jit(solution)/shard_map/ppermute | solution.py:31
  67.8 5.4 %collective-permute-start.27 = (bf16[64,512]{1,0:T(8,128)(2,1)S(1)}, bf16[64,512]{1,0:T(8,128)(2,1)S(1)}, u32[]{:S(2)}, u32[]{:S(2)}) collective-permute-start(bf16[64,512]{1,0:T(8,128)(2,1)S(1)} %add_convert_fusion.3), channel_id=1, source_target_pairs={{0,1},{1,0},{2,3},{3,2},{4,5},{5,4},{6,7},{7,6},{8,9},{9,8},{10,11... | collective-permute-start | bytes 196616 | tf_op jit(solution)/shard_map/ppermute | solution.py:21
  69.7 5.7 %collective-permute-start.18 = (bf16[8,7296]{1,0:T(8,128)(2,1)S(1)}, bf16[8,7296]{1,0:T(8,128)(2,1)S(1)}, u32[]{:S(2)}, u32[]{:S(2)}) collective-permute-start(bf16[8,7296]{1,0:T(8,128)(2,1)S(1)} %get-tuple-element.40), channel_id=1, source_target_pairs={{0,8},{4,20},{8,0},{12,28},{16,24},{20,4},{24,16},{28,12},{1,9},{5... | collective-permute-start | bytes 350216 | tf_op jit(solution)/shard_map/ppermute | solution.py:31
  71.0 7.0 %collective-permute-start.19 = (bf16[8,7296]{1,0:T(8,128)(2,1)S(1)}, bf16[8,7296]{1,0:T(8,128)(2,1)S(1)}, u32[]{:S(2)}, u32[]{:S(2)}) collective-permute-start(bf16[8,7296]{1,0:T(8,128)(2,1)S(1)} %get-tuple-element.41), channel_id=1, source_target_pairs={{0,16},{4,12},{8,24},{12,4},{16,0},{20,28},{24,8},{28,20},{1,17},{... | collective-permute-start | bytes 350216 | tf_op jit(solution)/shard_map/ppermute | solution.py:31
  71.6 6.4 %collective-permute-start.20 = (bf16[8,7296]{1,0:T(8,128)(2,1)S(1)}, bf16[8,7296]{1,0:T(8,128)(2,1)S(1)}, u32[]{:S(2)}, u32[]{:S(2)}) collective-permute-start(bf16[8,7296]{1,0:T(8,128)(2,1)S(1)} %get-tuple-element.42), channel_id=1, source_target_pairs={{0,24},{4,28},{8,16},{12,20},{16,8},{20,12},{24,0},{28,4},{1,25},{... | collective-permute-start | bytes 350216 | tf_op jit(solution)/shard_map/ppermute | solution.py:31
  73.3 9.2 %collective-permute-start.28 = (bf16[64,512]{1,0:T(8,128)(2,1)S(1)}, bf16[64,512]{1,0:T(8,128)(2,1)S(1)}, u32[]{:S(2)}, u32[]{:S(2)}) collective-permute-start(bf16[64,512]{1,0:T(8,128)(2,1)S(1)} %add_convert_fusion.2.refs_7_), channel_id=1, source_target_pairs={{0,2},{1,3},{2,0},{3,1},{4,6},{5,7},{6,4},{7,5},{8,10},{9,11},{10,... | collective-permute-start | bytes 196616 | tf_op jit(solution)/shard_map/ppermute | solution.py:21
  78.1 4.4 %collective-permute-start.21 = (bf16[2,7296]{1,0:T(2,128)(2,1)S(1)}, bf16[2,7296]{1,0:T(2,128)(2,1)S(1)}, u32[]{:S(2)}, u32[]{:S(2)}) collective-permute-start(bf16[2,7296]{1,0:T(2,128)(2,1)S(1)} %get-tuple-element.44), channel_id=1, source_target_pairs={{0,1},{1,0},{2,3},{3,2},{4,5},{5,4},{6,7},{7,6},{8,9},{9,8},{10,11... | collective-permute-start | bytes 87560 | tf_op jit(solution)/shard_map/ppermute | solution.py:21
  78.5 4.8 %collective-permute-start.22 = (bf16[2,7296]{1,0:T(2,128)(2,1)S(1)}, bf16[2,7296]{1,0:T(2,128)(2,1)S(1)}, u32[]{:S(2)}, u32[]{:S(2)}) collective-permute-start(bf16[2,7296]{1,0:T(2,128)(2,1)S(1)} %get-tuple-element.45), channel_id=1, source_target_pairs={{0,2},{1,3},{2,0},{3,1},{4,6},{5,7},{6,4},{7,5},{8,10},{9,11},{10,... | collective-permute-start | bytes 87560 | tf_op jit(solution)/shard_map/ppermute | solution.py:21
  81.4 5.7 %collective-permute-start.23 = (bf16[2,7296]{1,0:T(2,128)(2,1)S(1)}, bf16[2,7296]{1,0:T(2,128)(2,1)S(1)}, u32[]{:S(2)}, u32[]{:S(2)}) collective-permute-start(bf16[2,7296]{1,0:T(2,128)(2,1)S(1)} %get-tuple-element.46), channel_id=1, source_target_pairs={{0,3},{1,2},{2,1},{3,0},{4,7},{5,6},{6,5},{7,4},{8,11},{9,10},{10,... | collective-permute-start | bytes 87560 | tf_op jit(solution)/shard_map/ppermute | solution.py:21

commit v2 on v1

--- a/solution.py
+++ b/solution.py
@@ -153,6 +153,30 @@
         flops=4 * n_exp * CAP * rows * width,
     )
     return res[:n_exp], res[n_exp], res[n_exp + 1]
+
+
+def pack_body(*refs):
+    msgs, out = refs[:-1], refs[-1]
+    width = out.shape[1]
+    step = 1024
+    for c in range(width // step):
+        cols = pl.ds(c * step, step)
+        held = [msg[:, cols].astype(F32) for msg in msgs]
+        parts = [h[:CAP] for h in held] + [h[CAP:] for h in held]
+        out[:, cols] = jnp.concatenate(parts, axis=0).astype(BF16)
+
+
+def pack(msgs):
+    width = msgs[0].shape[1]
+    (rows,) = call(
+        pack_body,
+        [jax.ShapeDtypeStruct((2 * CAP * len(msgs), width), BF16)],
+        tuple(msgs),
+        [vmem_spec()] * len(msgs),
+        [],
+        4 * MIB,
+    )
+    return rows
 
 
 def attention_body(n_blocks, heads, row_block, *refs):
@@ -376,11 +400,7 @@
 
 def final_body(n_exp, chunks, *refs):
     msgs = refs[:n_exp]
-    weight_ref, chosen_ref, ids_ref, mine_ref, other_ref = refs[n_exp : n_exp + 5]
-    dtok_hbm, dgate_ref, dlat_hbm, out, dlat, sems = refs[n_exp + 5 :]
-    dlat[...] = (mine_ref[...].astype(F32) + other_ref[...].astype(F32)).astype(BF16)
-    dlat_write = pltpu.make_async_copy(dlat, dlat_hbm, sems.at[chunks])
-    dlat_write.start()
+    weight_ref, chosen_ref, ids_ref, dtok_hbm, dgate_ref, out, sems = refs[n_exp:]
     width = msgs[0].shape[1] - LANES
     top, rows = ids_ref.shape
     slots = n_exp * CAP
@@ -392,7 +412,7 @@
     lhs = jnp.concatenate([high, mid, low], axis=0)
     tn = (((0,), (0,)), ((), ()))
     step = width // chunks
-    writes = [dlat_write]
+    writes = []
     for c in range(chunks):
         cols = pl.ds(c * step, step)
         piece = jnp.concatenate([msg[:, cols] for msg in msgs], axis=0)
@@ -414,30 +434,28 @@
         write.wait()
 
 
-def final(msgs, weight, chosen, expert_ids, lat_mine, lat_other):
+def final(msgs, weight, chosen, expert_ids):
     n_exp = len(msgs)
     width = msgs[0].shape[1] - LANES
     rows, top = expert_ids.shape
     chunks = 7
-    d_tokens, d_gates, d_latent = call(
+    d_tokens, d_gates = call(
         functools.partial(final_body, n_exp, chunks),
         [
             jax.ShapeDtypeStruct((rows, width), BF16),
             jax.ShapeDtypeStruct((top, rows), BF16),
-            jax.ShapeDtypeStruct(lat_mine.shape, BF16),
         ],
-        (*msgs, weight, chosen, expert_ids.T, lat_mine, lat_other),
-        [vmem_spec()] * (n_exp + 5),
+        (*msgs, weight, chosen, expert_ids.T),
+        [vmem_spec()] * (n_exp + 3),
         [
             pltpu.VMEM((rows, width), BF16),
-            pltpu.VMEM(lat_mine.shape, BF16),
-            pltpu.SemaphoreType.DMA((chunks + 1,)),
+            pltpu.SemaphoreType.DMA((chunks,)),
         ],
         12 * MIB,
         flops=6 * n_exp * CAP * rows * width,
-        out_specs=[hbm_spec(), vmem_spec(), hbm_spec()],
-    )
-    return d_tokens, d_gates.T, d_latent
+        out_specs=[hbm_spec(), vmem_spec()],
+    )
+    return d_tokens, d_gates.T
 
 
 def gather_blocks(own, n_ctx):
@@ -477,7 +495,7 @@
         expert_ids, gate_order, gate_values, tokens, token_grads, n_exp
     )
     got = [sends[0]] + [exchange(sends[k], "exp", k) for k in range(1, n_exp)]
-    own_rows = jnp.concatenate([g[:CAP] for g in got] + [g[CAP:] for g in got], axis=0)
+    own_rows = pack(got)
 
     doc_cols = jnp.broadcast_to(doc_ids.astype(BF16)[:, None], (per_dev, LANES))
     lat_blocks = gather_blocks(jnp.concatenate([latent, doc_cols], axis=1), n_ctx)
@@ -502,9 +520,8 @@
     parts = [summed[0]] + [chip_exchange(summed[p], p) for p in range(1, chips)]
     backs = owner_sum(parts, n_exp)
     back = [backs[0]] + [exchange(backs[k], "exp", k) for k in range(1, n_exp)]
-    d_tokens, d_gates, d_latent = final(
-        back, weight, chosen, expert_ids, lat_total, lat_other
-    )
+    d_tokens, d_gates = final(back, weight, chosen, expert_ids)
+    d_latent = widen_add(lat_total, lat_other)
     return (d_queries, d_latent, d_tokens, d_gates)
 
 

time: 89.5 us -> 71.7 us (0.80)
  local copies, waits for them, and re-layouts: 12.2 us -> 0.1 us
  waiting for transfers between devices: 29.4 us -> 23.7 us
    unnamed x18 -> x6, local copies, waits for them, and re-layouts: 11.6 us -> 0.01 us
    ppermute x18, waiting for transfers between devices: 14.2 us -> 4.22 us  [exchange(): return lax.ppermute(array, axis, [(i, i ^ mask) for i in range(count)])]
    ppermute x11, waiting for transfers between devices: 15.3 us -> 19.5 us  [chip_exchange(): return lax.ppermute(array, 'ctx', pairs)]
    pallas_call x6 -> x7, Pallas kernels: 16 us -> 16.1 us  [call(): pl.pallas_call(body, out_shape=outs, in_specs=in_specs, out_specs=out_spe...]
  transfers between devices with their start and end apart: 29 -> 29, of which waited for: 13 -> 10; matrix products, arithmetic and copies ran while one was open for 1% -> 1% of each run, Pallas kernels for 16% -> 20%
where the time goes in v2:
time: 71.7 us; the launch traced here: 71.5 us
  starting transfers between devices  28.4 us (40%)
  waiting for transfers between devices  23.7 us (33%)
  Pallas kernels  16.1 us (22%)
  other arithmetic  2.44 us (3%)
  between operations  0.78 us (1%)
    ppermute x11, waiting for transfers between devices, chip_exchange(): return lax.ppermute(array, 'ctx', pairs)  19.5 us
    pallas_call x7, Pallas kernels, call(): pl.pallas_call(body, out_shape=outs, in_specs=in_specs, out_specs=out_spe...  16.1 us
    ppermute x18, starting transfers between devices, exchange(): return lax.ppermute(array, axis, [(i, i ^ mask) for i in range(count)])  14.5 us
    ppermute x11, starting transfers between devices, chip_exchange(): return lax.ppermute(array, 'ctx', pairs)  13.8 us
    ppermute x18, waiting for transfers between devices, exchange(): return lax.ppermute(array, axis, [(i, i ^ mask) for i in range(count)])  4.22 us
  transfers between devices with their start and end apart: 29, of which 10 were waited for; matrix products, arithmetic and copies ran while one was open for 1% of the time, Pallas kernels for 20%

profile of v2, /device:TPU:0, one launch (start us, length us, event | category | flops | bytes accessed | tf_op | source)
XLA Modules:
  0.0 71.5 jit_solution(4799731634060087908)
XLA Ops:
  0.7 0.8 %convert_element_type.48 = bf16[64]{0:T(256)(128)(2,1)S(1)} convert(s32[64]{0:T(128)} %param.15) | non-fusion elementwise | flops 64 | bytes 384 | tf_op jit(solution)/shard_map/convert_element_type | solution.py:500
  1.5 0.1 broadcast_in_dim.2
  1.5 0.9 %pad_maximum_fusion.refs_2_ = bf16[64,640]{1,0:T(8,128)(2,1)S(1)} fusion(bf16[64,128]{1,0:T(8,128)(2,1)S(1)} %broadcast_in_dim.2, bf16[64,512]{1,0:T(8,128)(2,1)} %param.13), kind=kLoop, calls=%fused_computation.5 | loop fusion | flops 163840 | bytes 163840 | tf_op jit(solution)/shard_map/concatenate | solution.py:501
  2.4 3.0 %collective-permute-start = (bf16[64,640]{1,0:T(8,128)(2,1)S(1)}, bf16[64,640]{1,0:T(8,128)(2,1)S(1)}, u32[]{:S(2)}, u32[]{:S(2)}) collective-permute-start(bf16[64,640]{1,0:T(8,128)(2,1)S(1)} %pad_maximum_fusion.refs_2_), channel_id=1, source_target_pairs={{0,8},{4,20},{8,0},{12,28},{16,24},{20,4},{24,16},{28,12},{1,9},{5... | collective-permute-start | bytes 245768 | tf_op jit(solution)/shard_map/ppermute | solution.py:31
  5.4 1.5 %collective-permute-start.1 = (bf16[64,640]{1,0:T(8,128)(2,1)S(1)}, bf16[64,640]{1,0:T(8,128)(2,1)S(1)}, u32[]{:S(2)}, u32[]{:S(2)}) collective-permute-start(bf16[64,640]{1,0:T(8,128)(2,1)S(1)} %pad_maximum_fusion.refs_2_), channel_id=1, source_target_pairs={{0,16},{4,12},{8,24},{12,4},{16,0},{20,28},{24,8},{28,20},{1,17},{... | collective-permute-start | bytes 245768 | tf_op jit(solution)/shard_map/ppermute | solution.py:31
  6.9 0.0 collective-permute-start.2
  6.9 0.0 collective-permute-start.3
  6.9 1.2 %collective-permute-done.refs_3_ = bf16[64,640]{1,0:T(8,128)(2,1)S(1)} collective-permute-done((bf16[64,640]{1,0:T(8,128)(2,1)S(1)}, bf16[64,640]{1,0:T(8,128)(2,1)S(1)}, u32[]{:S(2)}, u32[]{:S(2)}) %collective-permute-start) | collective-permute-done | bytes 81952 | tf_op jit(solution)/shard_map/ppermute | solution.py:31
  8.1 0.0 collective-permute-start.4
  8.1 2.6 %collective-permute-done.1.refs_4_ = bf16[64,640]{1,0:T(8,128)(2,1)S(1)} collective-permute-done((bf16[64,640]{1,0:T(8,128)(2,1)S(1)}, bf16[64,640]{1,0:T(8,128)(2,1)S(1)}, u32[]{:S(2)}, u32[]{:S(2)}) %collective-permute-start.1) | collective-permute-done | bytes 81952 | tf_op jit(solution)/shard_map/ppermute | solution.py:31
  10.7 0.0 collective-permute-start.5
  10.7 1.5 %collective-permute-done.2.refs_5_ = bf16[64,640]{1,0:T(8,128)(2,1)S(1)} collective-permute-done((bf16[64,640]{1,0:T(8,128)(2,1)S(1)}, bf16[64,640]{1,0:T(8,128)(2,1)S(1)}, u32[]{:S(2)}, u32[]{:S(2)}) %collective-permute-start.2) | collective-permute-done | bytes 81952 | tf_op jit(solution)/shard_map/ppermute | solution.py:31
  12.2 0.0 collective-permute-start.6
  12.2 2.4 %shard_map.148 = (bf16[4,7168]{1,0:T(4,128)(2,1)S(1)}, bf16[4,7168]{1,0:T(4,128)(2,1)S(1)}, bf16[4,7168]{1,0:T(4,128)(2,1)S(1)}, bf16[4,7168]{1,0:T(4,128)(2,1)S...) custom-call(s32[8,128]{1,0:T(8,128)} %bitcast.8, s32[1,128]{1,0:T(1,128)} %order_hbm.1, f32[8,128]{1,0:T(8,128)} %bitcast.10, ...), custom_call_target="tpu_custom_call" | custom-call | flops 29360128 | bytes 3916288 | tf_op jit(solution)/shard_map/pallas_call | solution.py:60
  14.6 1.6 %collective-permute-start.12 = (bf16[4,7168]{1,0:T(4,128)(2,1)S(1)}, bf16[4,7168]{1,0:T(4,128)(2,1)S(1)}, u32[]{:S(2)}, u32[]{:S(2)}) collective-permute-start(bf16[4,7168]{1,0:T(4,128)(2,1)S(1)} %get-tuple-element.32), channel_id=1, source_target_pairs={{0,1},{1,0},{2,3},{3,2},{4,5},{5,4},{6,7},{7,6},{8,9},{9,8},{10,11... | collective-permute-start | bytes 172040 | tf_op jit(solution)/shard_map/ppermute | solution.py:21
  16.2 0.0 collective-permute-done.3.refs_6_
  16.2 2.6 %collective-permute-start.13 = (bf16[4,7168]{1,0:T(4,128)(2,1)S(1)}, bf16[4,7168]{1,0:T(4,128)(2,1)S(1)}, u32[]{:S(2)}, u32[]{:S(2)}) collective-permute-start(bf16[4,7168]{1,0:T(4,128)(2,1)S(1)} %get-tuple-element.33), channel_id=1, source_target_pairs={{0,2},{1,3},{2,0},{3,1},{4,6},{5,7},{6,4},{7,5},{8,10},{9,11},{10,... | collective-permute-start | bytes 172040 | tf_op jit(solution)/shard_map/ppermute | solution.py:21
  18.8 0.2 collective-permute-start.14
  19.1 0.0 collective-permute-done.5.refs_8_
  19.1 0.0 collective-permute-done.6.refs_9_
  19.1 5.2 %shard_map.147 = (bf16[1024,512]{1,0:T(8,128)(2,1)}, bf16[256,512]{1,0:T(8,128)(2,1)S(1)}, bf16[256,512]{1,0:T(8,128)(2,1)S(1)}, bf16[7168,256]{1,0:T(8,128)(2,1...) custom-call(bf16[1024,512]{1,0:T(8,128)(2,1)S(1)} %bitcast.6, bf16[1024,512]{1,0:T(8,128)(2,1)S(1)} %bitcast.7, ...), custom_call_target="tpu_custom_call" | custom-call | flops 2684354560 | bytes 26345472 | tf_op jit(solution)/shard_map/pallas_call | solution.py:60
  24.3 0.1 collective-permute-start.7
  24.4 0.0 collective-permute-done.12.refs_1_
  24.4 0.4 collective-permute-done.14.refs_3_
  24.8 0.1 shard_map.149.refs_0_
  24.9 0.6 collective-permute-start.15
  25.5 1.1 %collective-permute-start.16 = (bf16[16,7168]{1,0:T(8,128)(2,1)S(1)}, bf16[16,7168]{1,0:T(8,128)(2,1)S(1)}, u32[]{:S(2)}, u32[]{:S(2)}) collective-permute-start(bf16[16,7168]{1,0:T(8,128)(2,1)S(1)} %shard_map.149.refs_0_), channel_id=1, source_target_pairs={{0,16},{4,12},{8,24},{12,4},{16,0},{20,28},{24,8},{28,20},{1,17},{... | collective-permute-start | bytes 688136 | tf_op jit(solution)/shard_map/ppermute | solution.py:31
  26.7 1.8 %collective-permute-start.17 = (bf16[16,7168]{1,0:T(8,128)(2,1)S(1)}, bf16[16,7168]{1,0:T(8,128)(2,1)S(1)}, u32[]{:S(2)}, u32[]{:S(2)}) collective-permute-start(bf16[16,7168]{1,0:T(8,128)(2,1)S(1)} %shard_map.149.refs_0_), channel_id=1, source_target_pairs={{0,24},{4,28},{8,16},{12,20},{16,8},{20,12},{24,0},{28,4},{1,25},{... | collective-permute-start | bytes 688136 | tf_op jit(solution)/shard_map/ppermute | solution.py:31
  28.5 0.0 collective-permute-start.18
  28.5 5.0 %collective-permute-done.15.refs_1_ = bf16[16,7168]{1,0:T(8,128)(2,1)S(1)} collective-permute-done((bf16[16,7168]{1,0:T(8,128)(2,1)S(1)}, bf16[16,7168]{1,0:T(8,128)(2,1)S(1)}, u32[]{:S(2)}, u32[]{:S(2)}) %collective-permute-start.15) | collective-permute-done | bytes 229408 | tf_op jit(solution)/shard_map/ppermute | solution.py:31
  33.5 0.0 collective-permute-start.19
  33.5 0.0 collective-permute-done.16.refs_2_
  33.5 0.5 collective-permute-start.20
  34.0 4.7 %collective-permute-done.17.refs_3_ = bf16[16,7168]{1,0:T(8,128)(2,1)S(1)} collective-permute-done((bf16[16,7168]{1,0:T(8,128)(2,1)S(1)}, bf16[16,7168]{1,0:T(8,128)(2,1)S(1)}, u32[]{:S(2)}, u32[]{:S(2)}) %collective-permute-start.17) | collective-permute-done | bytes 229408 | tf_op jit(solution)/shard_map/ppermute | solution.py:31
  38.7 0.0 collective-permute-start.21
  38.7 0.1 add_convert_fusion
  38.8 1.3 %collective-permute-start.8 = (bf16[128,512]{1,0:T(8,128)(2,1)S(1)}, bf16[128,512]{1,0:T(8,128)(2,1)S(1)}, u32[]{:S(2)}, u32[]{:S(2)}) collective-permute-start(bf16[128,512]{1,0:T(8,128)(2,1)S(1)} %slice.17), channel_id=1, source_target_pairs={{0,16},{4,12},{8,24},{12,4},{16,0},{20,28},{24,8},{28,20},{1,17},{... | collective-permute-start | bytes 393224 | tf_op jit(solution)/shard_map/ppermute | solution.py:31
  40.1 0.0 collective-permute-done.18.refs_4_
  40.1 0.0 collective-permute-done.19.refs_5_
  40.1 0.0 collective-permute-done.20.refs_6_
  40.1 0.0 collective-permute-done.21.refs_7_
  40.2 6.0 %shard_map.150 = (bf16[32,7296]{1,0:T(8,128)(2,1)S(1)}, bf16[32,7296]{1,0:T(8,128)(2,1)S(1)}) custom-call(bf16[16,7168]{1,0:T(8,128)(2,1)S(1)} %shard_map.149.refs_0_, bf16[16,7168]{1,0:T(8,128)(2,1)S(1)} %collective-permute-done.15.refs_1_, bf16[16,7168]{1,0:T(8,128)(2,1)S(1)} %collective-permute-done.16.refs_2_, ...), custom_call_target="tpu_custom_call" | custom-call | flops 1174405120 | bytes 13778944 | tf_op jit(solution)/shard_map/pallas_call | solution.py:60
  46.2 0.2 collective-permute-start.22
  46.4 0.0 collective-permute-done.8
  46.4 0.9 %collective-permute-start.9 = (bf16[64,512]{1,0:T(8,128)(2,1)S(1)}, bf16[64,512]{1,0:T(8,128)(2,1)S(1)}, u32[]{:S(2)}, u32[]{:S(2)}) collective-permute-start(bf16[64,512]{1,0:T(8,128)(2,1)S(1)} %slice.19), channel_id=1, source_target_pairs={{0,8},{4,20},{8,0},{12,28},{16,24},{20,4},{24,16},{28,12},{1,9},{5... | collective-permute-start | bytes 196616 | tf_op jit(solution)/shard_map/ppermute | solution.py:31
  47.3 3.4 %collective-permute-done.9 = bf16[64,512]{1,0:T(8,128)(2,1)S(1)} collective-permute-done((bf16[64,512]{1,0:T(8,128)(2,1)S(1)}, bf16[64,512]{1,0:T(8,128)(2,1)S(1)}, u32[]{:S(2)}, u32[]{:S(2)}) %collective-permute-start.9) | collective-permute-done | bytes 65568 | tf_op jit(solution)/shard_map/ppermute | solution.py:31
  50.8 0.7 %collective-permute-start.10 = (bf16[64,512]{1,0:T(8,128)(2,1)S(1)}, bf16[64,512]{1,0:T(8,128)(2,1)S(1)}, u32[]{:S(2)}, u32[]{:S(2)}) collective-permute-start(bf16[64,512]{1,0:T(8,128)(2,1)S(1)} %add_convert_fusion.4), channel_id=1, source_target_pairs={{0,1},{1,0},{2,3},{3,2},{4,5},{5,4},{6,7},{7,6},{8,9},{9,8},{10,11... | collective-permute-start | bytes 196616 | tf_op jit(solution)/shard_map/ppermute | solution.py:21
  51.5 0.2 shard_map.151
  51.7 0.9 %collective-permute-start.23 = (bf16[8,7296]{1,0:T(8,128)(2,1)S(1)}, bf16[8,7296]{1,0:T(8,128)(2,1)S(1)}, u32[]{:S(2)}, u32[]{:S(2)}) collective-permute-start(bf16[8,7296]{1,0:T(8,128)(2,1)S(1)} %get-tuple-element.41), channel_id=1, source_target_pairs={{0,8},{4,20},{8,0},{12,28},{16,24},{20,4},{24,16},{28,12},{1,9},{5... | collective-permute-start | bytes 350216 | tf_op jit(solution)/shard_map/ppermute | solution.py:31
  52.6 1.0 %collective-permute-start.24 = (bf16[8,7296]{1,0:T(8,128)(2,1)S(1)}, bf16[8,7296]{1,0:T(8,128)(2,1)S(1)}, u32[]{:S(2)}, u32[]{:S(2)}) collective-permute-start(bf16[8,7296]{1,0:T(8,128)(2,1)S(1)} %get-tuple-element.42), channel_id=1, source_target_pairs={{0,16},{4,12},{8,24},{12,4},{16,0},{20,28},{24,8},{28,20},{1,17},{... | collective-permute-start | bytes 350216 | tf_op jit(solution)/shard_map/ppermute | solution.py:31
  53.5 1.7 %collective-permute-start.25 = (bf16[8,7296]{1,0:T(8,128)(2,1)S(1)}, bf16[8,7296]{1,0:T(8,128)(2,1)S(1)}, u32[]{:S(2)}, u32[]{:S(2)}) collective-permute-start(bf16[8,7296]{1,0:T(8,128)(2,1)S(1)} %get-tuple-element.43), channel_id=1, source_target_pairs={{0,24},{4,28},{8,16},{12,20},{16,8},{20,12},{24,0},{28,4},{1,25},{... | collective-permute-start | bytes 350216 | tf_op jit(solution)/shard_map/ppermute | solution.py:31
  55.2 0.0 collective-permute-done.10
  55.3 3.6 %collective-permute-start.11 = (bf16[64,512]{1,0:T(8,128)(2,1)S(1)}, bf16[64,512]{1,0:T(8,128)(2,1)S(1)}, u32[]{:S(2)}, u32[]{:S(2)}) collective-permute-start(bf16[64,512]{1,0:T(8,128)(2,1)S(1)} %add_convert_fusion.3), channel_id=1, source_target_pairs={{0,2},{1,3},{2,0},{3,1},{4,6},{5,7},{6,4},{7,5},{8,10},{9,11},{10,... | collective-permute-start | bytes 196616 | tf_op jit(solution)/shard_map/ppermute | solution.py:21
  58.8 0.0 collective-permute-done.23.refs_1_
  58.8 1.1 %collective-permute-done.24.refs_2_ = bf16[8,7296]{1,0:T(8,128)(2,1)S(1)} collective-permute-done((bf16[8,7296]{1,0:T(8,128)(2,1)S(1)}, bf16[8,7296]{1,0:T(8,128)(2,1)S(1)}, u32[]{:S(2)}, u32[]{:S(2)}) %collective-permute-start.24) | collective-permute-done | bytes 116768 | tf_op jit(solution)/shard_map/ppermute | solution.py:31
  59.9 0.1 shard_map.152
  60.0 1.4 %collective-permute-start.26 = (bf16[2,7296]{1,0:T(2,128)(2,1)S(1)}, bf16[2,7296]{1,0:T(2,128)(2,1)S(1)}, u32[]{:S(2)}, u32[]{:S(2)}) collective-permute-start(bf16[2,7296]{1,0:T(2,128)(2,1)S(1)} %get-tuple-element.45), channel_id=1, source_target_pairs={{0,1},{1,0},{2,3},{3,2},{4,5},{5,4},{6,7},{7,6},{8,9},{9,8},{10,11... | collective-permute-start | bytes 87560 | tf_op jit(solution)/shard_map/ppermute | solution.py:21
  61.4 2.3 %collective-permute-start.27 = (bf16[2,7296]{1,0:T(2,128)(2,1)S(1)}, bf16[2,7296]{1,0:T(2,128)(2,1)S(1)}, u32[]{:S(2)}, u32[]{:S(2)}) collective-permute-start(bf16[2,7296]{1,0:T(2,128)(2,1)S(1)} %get-tuple-element.46), channel_id=1, source_target_pairs={{0,2},{1,3},{2,0},{3,1},{4,6},{5,7},{6,4},{7,5},{8,10},{9,11},{10,... | collective-permute-start | bytes 87560 | tf_op jit(solution)/shard_map/ppermute | solution.py:21
  63.7 1.3 %collective-permute-start.28 = (bf16[2,7296]{1,0:T(2,128)(2,1)S(1)}, bf16[2,7296]{1,0:T(2,128)(2,1)S(1)}, u32[]{:S(2)}, u32[]{:S(2)}) collective-permute-start(bf16[2,7296]{1,0:T(2,128)(2,1)S(1)} %get-tuple-element.47), channel_id=1, source_target_pairs={{0,3},{1,2},{2,1},{3,0},{4,7},{5,6},{6,5},{7,4},{8,11},{9,10},{10,... | collective-permute-start | bytes 87560 | tf_op jit(solution)/shard_map/ppermute | solution.py:21
  65.0 0.6 add_convert_fusion.2
  65.7 0.0 collective-permute-done.26.refs_1_
  65.7 0.5 collective-permute-done.27.refs_2_
  66.2 3.2 %collective-permute-done.28.refs_3_ = bf16[2,7296]{1,0:T(2,128)(2,1)S(1)} collective-permute-done((bf16[2,7296]{1,0:T(2,128)(2,1)S(1)}, bf16[2,7296]{1,0:T(2,128)(2,1)S(1)}, u32[]{:S(2)}, u32[]{:S(2)}) %collective-permute-start.28) | collective-permute-done | bytes 29216 | tf_op jit(solution)/shard_map/ppermute | solution.py:21
  69.4 2.1 %shard_map.153 = (bf16[128,7168]{1,0:T(8,128)(2,1)}, bf16[8,128]{1,0:T(8,128)(2,1)}) custom-call(bf16[2,7296]{1,0:T(2,128)(2,1)S(1)} %get-tuple-element.44.refs_0_, bf16[2,7296]{1,0:T(2,128)(2,1)S(1)} %collective-permute-done.26.refs_1_, bf16[2,7296]{1,0:T(2,128)(2,1)S(1)} %collective-permute-done.27.refs_2_, ...), custom_call_target="tpu_custom_call" | custom-call | flops 44040192 | bytes 1966080 | tf_op jit(solution)/shard_map/pallas_call | solution.py:60
  (17 shorter events, 0.1 us)
Async XLA Ops:
  0.6 18.4 %copy-start = (bf16[64,16,512]{2,1,0:T(8,128)(2,1)S(1)}, bf16[64,16,512]{2,1,0:T(8,128)(2,1)}, u32[]{:S(2)}) copy-start(bf16[64,16,512]{2,1,0:T(8,128)(2,1)} %param.12) | copy-start | bytes 3145732
  0.6 18.4 %copy-start.1 = (bf16[64,16,512]{2,1,0:T(8,128)(2,1)S(1)}, bf16[64,16,512]{2,1,0:T(8,128)(2,1)}, u32[]{:S(2)}) copy-start(bf16[64,16,512]{2,1,0:T(8,128)(2,1)} %param.14) | copy-start | bytes 3145732
  2.4 5.7 %collective-permute-start = (bf16[64,640]{1,0:T(8,128)(2,1)S(1)}, bf16[64,640]{1,0:T(8,128)(2,1)S(1)}, u32[]{:S(2)}, u32[]{:S(2)}) collective-permute-start(bf16[64,640]{1,0:T(8,128)(2,1)S(1)} %pad_maximum_fusion.refs_2_), channel_id=1, source_target_pairs={{0,8},{4,20},{8,0},{12,28},{16,24},{20,4},{24,16},{28,12},{1,9},{5... | collective-permute-start | bytes 245768 | tf_op jit(solution)/shard_map/ppermute | solution.py:31
  5.4 5.3 %collective-permute-start.1 = (bf16[64,640]{1,0:T(8,128)(2,1)S(1)}, bf16[64,640]{1,0:T(8,128)(2,1)S(1)}, u32[]{:S(2)}, u32[]{:S(2)}) collective-permute-start(bf16[64,640]{1,0:T(8,128)(2,1)S(1)} %pad_maximum_fusion.refs_2_), channel_id=1, source_target_pairs={{0,16},{4,12},{8,24},{12,4},{16,0},{20,28},{24,8},{28,20},{1,17},{... | collective-permute-start | bytes 245768 | tf_op jit(solution)/shard_map/ppermute | solution.py:31
  6.9 5.3 %collective-permute-start.2 = (bf16[64,640]{1,0:T(8,128)(2,1)S(1)}, bf16[64,640]{1,0:T(8,128)(2,1)S(1)}, u32[]{:S(2)}, u32[]{:S(2)}) collective-permute-start(bf16[64,640]{1,0:T(8,128)(2,1)S(1)} %pad_maximum_fusion.refs_2_), channel_id=1, source_target_pairs={{0,24},{4,28},{8,16},{12,20},{16,8},{20,12},{24,0},{28,4},{1,25},{... | collective-permute-start | bytes 245768 | tf_op jit(solution)/shard_map/ppermute | solution.py:31
  6.9 9.4 %collective-permute-start.3 = (bf16[64,640]{1,0:T(8,128)(2,1)S(1)}, bf16[64,640]{1,0:T(8,128)(2,1)S(1)}, u32[]{:S(2)}, u32[]{:S(2)}) collective-permute-start(bf16[64,640]{1,0:T(8,128)(2,1)S(1)} %pad_maximum_fusion.refs_2_), channel_id=1, source_target_pairs={{0,4},{4,0},{8,12},{12,8},{16,20},{20,16},{24,28},{28,24},{1,5},{5... | collective-permute-start | bytes 245768 | tf_op jit(solution)/shard_map/ppermute | solution.py:21
  8.1 10.8 %collective-permute-start.4 = (bf16[64,640]{1,0:T(8,128)(2,1)S(1)}, bf16[64,640]{1,0:T(8,128)(2,1)S(1)}, u32[]{:S(2)}, u32[]{:S(2)}) collective-permute-start(bf16[64,640]{1,0:T(8,128)(2,1)S(1)} %collective-permute-done.refs_3_), channel_id=1, source_target_pairs={{0,4},{4,0},{8,12},{12,8},{16,20},{20,16},{24,28},{28,24},{1,5},{5... | collective-permute-start | bytes 245768 | tf_op jit(solution)/shard_map/ppermute | solution.py:21
  10.7 8.4 %collective-permute-start.5 = (bf16[64,640]{1,0:T(8,128)(2,1)S(1)}, bf16[64,640]{1,0:T(8,128)(2,1)S(1)}, u32[]{:S(2)}, u32[]{:S(2)}) collective-permute-start(bf16[64,640]{1,0:T(8,128)(2,1)S(1)} %collective-permute-done.1.refs_4_), channel_id=1, source_target_pairs={{0,4},{4,0},{8,12},{12,8},{16,20},{20,16},{24,28},{28,24},{1,5},{5... | collective-permute-start | bytes 245768 | tf_op jit(solution)/shard_map/ppermute | solution.py:21
  12.2 6.9 %collective-permute-start.6 = (bf16[64,640]{1,0:T(8,128)(2,1)S(1)}, bf16[64,640]{1,0:T(8,128)(2,1)S(1)}, u32[]{:S(2)}, u32[]{:S(2)}) collective-permute-start(bf16[64,640]{1,0:T(8,128)(2,1)S(1)} %collective-permute-done.2.refs_5_), channel_id=1, source_target_pairs={{0,4},{4,0},{8,12},{12,8},{16,20},{20,16},{24,28},{28,24},{1,5},{5... | collective-permute-start | bytes 245768 | tf_op jit(solution)/shard_map/ppermute | solution.py:21
  14.6 9.8 %collective-permute-start.12 = (bf16[4,7168]{1,0:T(4,128)(2,1)S(1)}, bf16[4,7168]{1,0:T(4,128)(2,1)S(1)}, u32[]{:S(2)}, u32[]{:S(2)}) collective-permute-start(bf16[4,7168]{1,0:T(4,128)(2,1)S(1)} %get-tuple-element.32), channel_id=1, source_target_pairs={{0,1},{1,0},{2,3},{3,2},{4,5},{5,4},{6,7},{7,6},{8,9},{9,8},{10,11... | collective-permute-start | bytes 172040 | tf_op jit(solution)/shard_map/ppermute | solution.py:21
  16.2 8.2 %collective-permute-start.13 = (bf16[4,7168]{1,0:T(4,128)(2,1)S(1)}, bf16[4,7168]{1,0:T(4,128)(2,1)S(1)}, u32[]{:S(2)}, u32[]{:S(2)}) collective-permute-start(bf16[4,7168]{1,0:T(4,128)(2,1)S(1)} %get-tuple-element.33), channel_id=1, source_target_pairs={{0,2},{1,3},{2,0},{3,1},{4,6},{5,7},{6,4},{7,5},{8,10},{9,11},{10,... | collective-permute-start | bytes 172040 | tf_op jit(solution)/shard_map/ppermute | solution.py:21
  18.8 6.0 %collective-permute-start.14 = (bf16[4,7168]{1,0:T(4,128)(2,1)S(1)}, bf16[4,7168]{1,0:T(4,128)(2,1)S(1)}, u32[]{:S(2)}, u32[]{:S(2)}) collective-permute-start(bf16[4,7168]{1,0:T(4,128)(2,1)S(1)} %get-tuple-element.34), channel_id=1, source_target_pairs={{0,3},{1,2},{2,1},{3,0},{4,7},{5,6},{6,5},{7,4},{8,11},{9,10},{10,... | collective-permute-start | bytes 172040 | tf_op jit(solution)/shard_map/ppermute | solution.py:21
  24.3 14.4 %collective-permute-start.7 = (bf16[256,512]{1,0:T(8,128)(2,1)S(1)}, bf16[256,512]{1,0:T(8,128)(2,1)S(1)}, u32[]{:S(2)}, u32[]{:S(2)}) collective-permute-start(bf16[256,512]{1,0:T(8,128)(2,1)S(1)} %get-tuple-element.30), channel_id=1, source_target_pairs={{0,4},{4,0},{8,12},{12,8},{16,20},{20,16},{24,28},{28,24},{1,5},{5... | collective-permute-start | bytes 786440 | tf_op jit(solution)/shard_map/ppermute | solution.py:21
  24.9 8.5 %collective-permute-start.15 = (bf16[16,7168]{1,0:T(8,128)(2,1)S(1)}, bf16[16,7168]{1,0:T(8,128)(2,1)S(1)}, u32[]{:S(2)}, u32[]{:S(2)}) collective-permute-start(bf16[16,7168]{1,0:T(8,128)(2,1)S(1)} %shard_map.149.refs_0_), channel_id=1, source_target_pairs={{0,8},{4,20},{8,0},{12,28},{16,24},{20,4},{24,16},{28,12},{1,9},{5... | collective-permute-start | bytes 688136 | tf_op jit(solution)/shard_map/ppermute | solution.py:31
  25.5 7.9 %collective-permute-start.16 = (bf16[16,7168]{1,0:T(8,128)(2,1)S(1)}, bf16[16,7168]{1,0:T(8,128)(2,1)S(1)}, u32[]{:S(2)}, u32[]{:S(2)}) collective-permute-start(bf16[16,7168]{1,0:T(8,128)(2,1)S(1)} %shard_map.149.refs_0_), channel_id=1, source_target_pairs={{0,16},{4,12},{8,24},{12,4},{16,0},{20,28},{24,8},{28,20},{1,17},{... | collective-permute-start | bytes 688136 | tf_op jit(solution)/shard_map/ppermute | solution.py:31
  26.7 12.0 %collective-permute-start.17 = (bf16[16,7168]{1,0:T(8,128)(2,1)S(1)}, bf16[16,7168]{1,0:T(8,128)(2,1)S(1)}, u32[]{:S(2)}, u32[]{:S(2)}) collective-permute-start(bf16[16,7168]{1,0:T(8,128)(2,1)S(1)} %shard_map.149.refs_0_), channel_id=1, source_target_pairs={{0,24},{4,28},{8,16},{12,20},{16,8},{20,12},{24,0},{28,4},{1,25},{... | collective-permute-start | bytes 688136 | tf_op jit(solution)/shard_map/ppermute | solution.py:31
  28.5 11.6 %collective-permute-start.18 = (bf16[16,7168]{1,0:T(8,128)(2,1)S(1)}, bf16[16,7168]{1,0:T(8,128)(2,1)S(1)}, u32[]{:S(2)}, u32[]{:S(2)}) collective-permute-start(bf16[16,7168]{1,0:T(8,128)(2,1)S(1)} %shard_map.149.refs_0_), channel_id=1, source_target_pairs={{0,4},{4,0},{8,12},{12,8},{16,20},{20,16},{24,28},{28,24},{1,5},{5... | collective-permute-start | bytes 688136 | tf_op jit(solution)/shard_map/ppermute | solution.py:21
  33.5 6.7 %collective-permute-start.19 = (bf16[16,7168]{1,0:T(8,128)(2,1)S(1)}, bf16[16,7168]{1,0:T(8,128)(2,1)S(1)}, u32[]{:S(2)}, u32[]{:S(2)}) collective-permute-start(bf16[16,7168]{1,0:T(8,128)(2,1)S(1)} %collective-permute-done.15.refs_1_), channel_id=1, source_target_pairs={{0,4},{4,0},{8,12},{12,8},{16,20},{20,16},{24,28},{28,24},{1,5},{5... | collective-permute-start | bytes 688136 | tf_op jit(solution)/shard_map/ppermute | solution.py:21
  33.5 6.6 %collective-permute-start.20 = (bf16[16,7168]{1,0:T(8,128)(2,1)S(1)}, bf16[16,7168]{1,0:T(8,128)(2,1)S(1)}, u32[]{:S(2)}, u32[]{:S(2)}) collective-permute-start(bf16[16,7168]{1,0:T(8,128)(2,1)S(1)} %collective-permute-done.16.refs_2_), channel_id=1, source_target_pairs={{0,4},{4,0},{8,12},{12,8},{16,20},{20,16},{24,28},{28,24},{1,5},{5... | collective-permute-start | bytes 688136 | tf_op jit(solution)/shard_map/ppermute | solution.py:21
  38.7 1.5 %collective-permute-start.21 = (bf16[16,7168]{1,0:T(8,128)(2,1)S(1)}, bf16[16,7168]{1,0:T(8,128)(2,1)S(1)}, u32[]{:S(2)}, u32[]{:S(2)}) collective-permute-start(bf16[16,7168]{1,0:T(8,128)(2,1)S(1)} %collective-permute-done.17.refs_3_), channel_id=1, source_target_pairs={{0,4},{4,0},{8,12},{12,8},{16,20},{20,16},{24,28},{28,24},{1,5},{5... | collective-permute-start | bytes 688136 | tf_op jit(solution)/shard_map/ppermute | solution.py:21
  38.8 7.6 %collective-permute-start.8 = (bf16[128,512]{1,0:T(8,128)(2,1)S(1)}, bf16[128,512]{1,0:T(8,128)(2,1)S(1)}, u32[]{:S(2)}, u32[]{:S(2)}) collective-permute-start(bf16[128,512]{1,0:T(8,128)(2,1)S(1)} %slice.17), channel_id=1, source_target_pairs={{0,16},{4,12},{8,24},{12,4},{16,0},{20,28},{24,8},{28,20},{1,17},{... | collective-permute-start | bytes 393224 | tf_op jit(solution)/shard_map/ppermute | solution.py:31
  40.2 29.2 %copy-start.2 = (s32[128,8]{0,1:T(8,128)S(1)}, s32[128,8]{0,1:T(8,128)}, u32[]{:S(2)}) copy-start(s32[128,8]{0,1:T(8,128)} %param.19) | copy-start | bytes 12292
  46.2 5.4 %collective-permute-start.22 = (bf16[32,7296]{1,0:T(8,128)(2,1)S(1)}, bf16[32,7296]{1,0:T(8,128)(2,1)S(1)}, u32[]{:S(2)}, u32[]{:S(2)}) collective-permute-start(bf16[32,7296]{1,0:T(8,128)(2,1)S(1)} %get-tuple-element.39), channel_id=1, source_target_pairs={{0,4},{4,0},{8,12},{12,8},{16,20},{20,16},{24,28},{28,24},{1,5},{5... | collective-permute-start | bytes 1400840 | tf_op jit(solution)/shard_map/ppermute | solution.py:21
  46.4 4.3 %collective-permute-start.9 = (bf16[64,512]{1,0:T(8,128)(2,1)S(1)}, bf16[64,512]{1,0:T(8,128)(2,1)S(1)}, u32[]{:S(2)}, u32[]{:S(2)}) collective-permute-start(bf16[64,512]{1,0:T(8,128)(2,1)S(1)} %slice.19), channel_id=1, source_target_pairs={{0,8},{4,20},{8,0},{12,28},{16,24},{20,4},{24,16},{28,12},{1,9},{5... | collective-permute-start | bytes 196616 | tf_op jit(solution)/shard_map/ppermute | solution.py:31
  50.8 4.5 %collective-permute-start.10 = (bf16[64,512]{1,0:T(8,128)(2,1)S(1)}, bf16[64,512]{1,0:T(8,128)(2,1)S(1)}, u32[]{:S(2)}, u32[]{:S(2)}) collective-permute-start(bf16[64,512]{1,0:T(8,128)(2,1)S(1)} %add_convert_fusion.4), channel_id=1, source_target_pairs={{0,1},{1,0},{2,3},{3,2},{4,5},{5,4},{6,7},{7,6},{8,9},{9,8},{10,11... | collective-permute-start | bytes 196616 | tf_op jit(solution)/shard_map/ppermute | solution.py:21
  51.7 7.1 %collective-permute-start.23 = (bf16[8,7296]{1,0:T(8,128)(2,1)S(1)}, bf16[8,7296]{1,0:T(8,128)(2,1)S(1)}, u32[]{:S(2)}, u32[]{:S(2)}) collective-permute-start(bf16[8,7296]{1,0:T(8,128)(2,1)S(1)} %get-tuple-element.41), channel_id=1, source_target_pairs={{0,8},{4,20},{8,0},{12,28},{16,24},{20,4},{24,16},{28,12},{1,9},{5... | collective-permute-start | bytes 350216 | tf_op jit(solution)/shard_map/ppermute | solution.py:31
  52.6 7.3 %collective-permute-start.24 = (bf16[8,7296]{1,0:T(8,128)(2,1)S(1)}, bf16[8,7296]{1,0:T(8,128)(2,1)S(1)}, u32[]{:S(2)}, u32[]{:S(2)}) collective-permute-start(bf16[8,7296]{1,0:T(8,128)(2,1)S(1)} %get-tuple-element.42), channel_id=1, source_target_pairs={{0,16},{4,12},{8,24},{12,4},{16,0},{20,28},{24,8},{28,20},{1,17},{... | collective-permute-start | bytes 350216 | tf_op jit(solution)/shard_map/ppermute | solution.py:31
  53.5 6.3 %collective-permute-start.25 = (bf16[8,7296]{1,0:T(8,128)(2,1)S(1)}, bf16[8,7296]{1,0:T(8,128)(2,1)S(1)}, u32[]{:S(2)}, u32[]{:S(2)}) collective-permute-start(bf16[8,7296]{1,0:T(8,128)(2,1)S(1)} %get-tuple-element.43), channel_id=1, source_target_pairs={{0,24},{4,28},{8,16},{12,20},{16,8},{20,12},{24,0},{28,4},{1,25},{... | collective-permute-start | bytes 350216 | tf_op jit(solution)/shard_map/ppermute | solution.py:31
  55.3 9.8 %collective-permute-start.11 = (bf16[64,512]{1,0:T(8,128)(2,1)S(1)}, bf16[64,512]{1,0:T(8,128)(2,1)S(1)}, u32[]{:S(2)}, u32[]{:S(2)}) collective-permute-start(bf16[64,512]{1,0:T(8,128)(2,1)S(1)} %add_convert_fusion.3), channel_id=1, source_target_pairs={{0,2},{1,3},{2,0},{3,1},{4,6},{5,7},{6,4},{7,5},{8,10},{9,11},{10,... | collective-permute-start | bytes 196616 | tf_op jit(solution)/shard_map/ppermute | solution.py:21
  60.0 5.6 %collective-permute-start.26 = (bf16[2,7296]{1,0:T(2,128)(2,1)S(1)}, bf16[2,7296]{1,0:T(2,128)(2,1)S(1)}, u32[]{:S(2)}, u32[]{:S(2)}) collective-permute-start(bf16[2,7296]{1,0:T(2,128)(2,1)S(1)} %get-tuple-element.45), channel_id=1, source_target_pairs={{0,1},{1,0},{2,3},{3,2},{4,5},{5,4},{6,7},{7,6},{8,9},{9,8},{10,11... | collective-permute-start | bytes 87560 | tf_op jit(solution)/shard_map/ppermute | solution.py:21
  61.4 4.8 %collective-permute-start.27 = (bf16[2,7296]{1,0:T(2,128)(2,1)S(1)}, bf16[2,7296]{1,0:T(2,128)(2,1)S(1)}, u32[]{:S(2)}, u32[]{:S(2)}) collective-permute-start(bf16[2,7296]{1,0:T(2,128)(2,1)S(1)} %get-tuple-element.46), channel_id=1, source_target_pairs={{0,2},{1,3},{2,0},{3,1},{4,6},{5,7},{6,4},{7,5},{8,10},{9,11},{10,... | collective-permute-start | bytes 87560 | tf_op jit(solution)/shard_map/ppermute | solution.py:21
  63.7 5.7 %collective-permute-start.28 = (bf16[2,7296]{1,0:T(2,128)(2,1)S(1)}, bf16[2,7296]{1,0:T(2,128)(2,1)S(1)}, u32[]{:S(2)}, u32[]{:S(2)}) collective-permute-start(bf16[2,7296]{1,0:T(2,128)(2,1)S(1)} %get-tuple-element.47), channel_id=1, source_target_pairs={{0,3},{1,2},{2,1},{3,0},{4,7},{5,6},{6,5},{7,4},{8,11},{9,10},{10,... | collective-permute-start | bytes 87560 | tf_op jit(solution)/shard_map/ppermute | solution.py:21
